TPU v7x, 32 devices: a whole 2x2x4 slice. The times are simulated.
32 devices in a mesh: outer: 8 (over z, y), narrow: 4 (over x, core).
Axes of the slice: x: 2, y: 2, z: 4, core: 2. Of those that a mesh axis runs over, the one named last changes fastest.
Arguments:
- queries: bfloat16 [8192, 4096], P(('outer', 'narrow')), may hold values from -6 to 6
- keys: bfloat16 [8192, 4096], P(('outer', 'narrow')), may hold values from -6 to 6
- values: bfloat16 [8192, 4096], P(('outer', 'narrow')), may hold values from -6 to 6
- log_decay: float32 [32, 8192], P(None, ('outer', 'narrow')), may hold values from -0.8 to 0
- gain: float32 [4096], replicated, may hold values from 0.5 to 1.5
Outputs:
- mixed: bfloat16 [8192, 4096], P(('outer', 'narrow'))
All inputs are finite; a program needn't handle non-finite values.
Results may differ from a plain program's by a relative error of at most 0.0052.
Values may be sent and summed in bfloat16 or wider, within the bound.
A program may use at most 64 MiB of HBM per device.

v0:
```python
import functools

import jax
import jax.numpy as jnp
from jax import lax
from jax.experimental import pallas as pl
from jax.experimental.pallas import tpu as pltpu
from jax.sharding import PartitionSpec as P

MESH = pl.DeviceIdType.MESH
FAR = -1e30


def split_outer(outer):
    rows = 1
    for d in range(1, outer + 1):
        if d * d <= outer and outer % d == 0:
            rows = d
    return outer // rows, rows


def kernel(
    sizes, q_hbm, k_hbm, v_hbm, ld_ref, gain_ref, out_ref,
    q_ref, k_ref, v_ref, cum, decay_cols, tail_cols, head_cols, bias, inner,
    made, got1, t1, wsend, got2, t2, got3, t3, gsend, got4, csend, carried,
    load_sem, send_sem, recv_sem, tsend_sem, trecv_sem,
):
    narrow, depth, rows, heads, width, unit = sizes
    tokens = q_ref.shape[0]
    own = heads // narrow
    chunks = own // rows
    o, n = lax.axis_index("outer"), lax.axis_index("narrow")
    z, y = o // rows, lax.rem(o, rows)

    near = [lax.rem(n + i % narrow, narrow) for i in range(narrow // 2, narrow // 2 + narrow) if i % narrow]
    level = [lax.rem(y + i, rows) for i in range(1, rows)]
    deep = [lax.rem(z + i, depth) for i in range(1, depth)]
    group_at = lambda j: (o, j)
    row_at = lambda j: (z * rows + j, n)
    depth_at = lambda j: (j * rows + y, n)

    loads = [
        pltpu.make_async_copy(src, dst, load_sem.at[i])
        for i, (src, dst) in enumerate(((k_hbm, k_ref), (v_hbm, v_ref), (q_hbm, q_ref)))
    ]
    for one in loads:
        one.start()

    barrier = pltpu.get_barrier_semaphore()
    peers = [group_at(j) for j in near] + [row_at(j) for j in level] + [depth_at(j) for j in deep]
    for peer in peers:
        pl.semaphore_signal(barrier, inc=1, device_id=peer, device_id_type=MESH)

    total = ld_ref[...]
    lane = lax.broadcasted_iota(jnp.int32, total.shape, 1)
    step = 1
    while step < tokens:
        total = total + jnp.where(lane >= step, pltpu.roll(total, step, axis=1), 0.0)
        step *= 2
    cum[...] = total
    t1[n] = jnp.broadcast_to(total[:, tokens - 1 :], (heads, width))
    cols = jnp.concatenate([total, jnp.zeros((128 - heads, tokens), jnp.float32)], axis=0).T
    tail = jnp.exp(cols[tokens - 1 :] - cols)
    grown = jnp.exp(cols)
    for g in range(heads // unit):
        shift = (128 - g * unit) % 128
        for ref, value in ((decay_cols, cols), (tail_cols, tail), (head_cols, grown)):
            ref[g] = pltpu.roll(value, shift, axis=1) if shift else value
    at_t = lax.broadcasted_iota(jnp.int32, (tokens, tokens), 0)
    at_s = lax.broadcasted_iota(jnp.int32, (tokens, tokens), 1)
    bias[...] = jnp.where(at_t >= at_s, 0.0, FAR)

    def lanes(h):
        return pl.ds(pl.multiple_of(h * width, width), width)

    def states(c):
        def body(j, _):
            for r in range(rows):
                k = c * rows + r
                at = lanes(j * own + k)
                tails = tail_cols[j * (own // unit) + k // unit]
                u = k % unit
                kept = k_ref[:, at].astype(jnp.float32) * tails[:, u : u + 1]
                made[c, j, r] = lax.dot_general(
                    kept.astype(jnp.bfloat16), v_ref[:, at], (((0,), (0,)), ((), ())),
                    preferred_element_type=jnp.float32,
                ).astype(jnp.bfloat16)
            return 0

        lax.fori_loop(0, narrow, body, 0, unroll=2)

    def within(first, last):
        def body(g, _):
            columns = decay_cols[g]
            for u in range(unit):
                h = g * unit + u
                at = lanes(h)
                scores = lax.dot_general(
                    q_ref[:, at], k_ref[:, at], (((1,), (1,)), ((), ())),
                    preferred_element_type=jnp.float32,
                )
                spread = columns[:, u : u + 1] - cum[pl.ds(h, 1), :] + bias[...]
                weights = (scores * jnp.exp(spread)).astype(jnp.bfloat16)
                inner[:, at] = jnp.dot(weights, v_ref[:, at], preferred_element_type=jnp.float32)
            return 0

        lax.fori_loop(first, last, body, 0)

    def finish(c, j):
        for r in range(rows):
            k = c * rows + r
            at = lanes(j * own + k)
            grow = head_cols[j * (own // unit) + k // unit]
            u = k % unit
            read = jnp.dot(q_ref[:, at], carried[c, j, r], preferred_element_type=jnp.float32)
            numer = inner[:, at] + read * grow[:, u : u + 1]
            mean = jnp.mean(numer * numer, axis=-1, keepdims=True)
            out_ref[:, at] = (numer * lax.rsqrt(mean + 1e-06) * gain_ref[:, at]).astype(jnp.bfloat16)

    pending = []

    def begin(kind, c, src, dst, peers_of, where, mine):
        for i, j in enumerate(peers_of):
            one = pltpu.make_async_remote_copy(
                src_ref=src(j), dst_ref=dst(mine), send_sem=send_sem.at[kind, c, i],
                recv_sem=recv_sem.at[kind, c, mine], device_id=where(j), device_id_type=MESH,
            )
            one.start()
            pending.append(one)

    def arrive(kind, c, dst, peers_of, where):
        for i, j in enumerate(peers_of):
            pltpu.make_async_remote_copy(
                src_ref=dst(j), dst_ref=dst(j), send_sem=send_sem.at[kind, c, i],
                recv_sem=recv_sem.at[kind, c, j], device_id=where(j), device_id_type=MESH,
            ).wait_recv()

    def begin_total(kind, ref, mine, peers_of, where):
        for i, j in enumerate(peers_of):
            one = pltpu.make_async_remote_copy(
                src_ref=ref.at[mine], dst_ref=ref.at[mine], send_sem=tsend_sem.at[kind, i],
                recv_sem=trecv_sem.at[kind, mine], device_id=where(j), device_id_type=MESH,
            )
            one.start()
            pending.append(one)

    def arrive_total(kind, ref, peers_of, where):
        for i, j in enumerate(peers_of):
            pltpu.make_async_remote_copy(
                src_ref=ref.at[j], dst_ref=ref.at[j], send_sem=tsend_sem.at[kind, i],
                recv_sem=trecv_sem.at[kind, j], device_id=where(j), device_id_type=MESH,
            ).wait_recv()

    def decay(ref, j, k):
        return jnp.exp(ref[j, pl.ds(n * own + k, 1), :])

    def stage0(c):
        states(c)
        begin(0, c, lambda j: made.at[c, j], lambda j: got1.at[c, j], near, group_at, n)
        got1[c, n] = made[c, n]

    def stage1(c):
        arrive(0, c, lambda j: got1.at[c, j], near, group_at)
        for r in range(rows):
            acc = got1[c, 0, r].astype(jnp.float32)
            for j in range(1, narrow):
                acc = decay(t1, j, c * rows + r) * acc + got1[c, j, r].astype(jnp.float32)
            wsend[c, r] = acc.astype(jnp.bfloat16)
        begin(1, c, lambda j: wsend.at[c, j], lambda j: got2.at[c, j], level, row_at, y)
        got2[c, y] = wsend[c, y]

    def stage2(c):
        arrive(1, c, lambda j: got2.at[c, j], level, row_at)
        acc = got2[c, 0].astype(jnp.float32)
        for j in range(1, rows):
            acc = decay(t2, j, c * rows + y) * acc + got2[c, j].astype(jnp.float32)
        got3[c, z] = acc.astype(jnp.bfloat16)
        begin(2, c, lambda j: got3.at[c, z], lambda j: got3.at[c, j], deep, depth_at, z)

    def stage3(c):
        arrive(2, c, lambda j: got3.at[c, j], deep, depth_at)
        k = c * rows + y
        acc = jnp.zeros((width, width), jnp.float32)
        for j in range(depth - 1):
            new = decay(t3, j, k) * acc + got3[c, j].astype(jnp.float32)
            acc = jnp.where(j < z, new, acc)
        for j in range(rows):
            gsend[c, j] = acc.astype(jnp.bfloat16)
            if j < rows - 1:
                acc = decay(t2, j, k) * acc + got2[c, j].astype(jnp.float32)
        begin(3, c, lambda j: gsend.at[c, j], lambda j: got4.at[c, j], level, row_at, y)
        got4[c, y] = gsend[c, y]

    def stage4(c):
        arrive(3, c, lambda j: got4.at[c, j], level, row_at)
        for r in range(rows):
            acc = got4[c, r].astype(jnp.float32)
            for j in range(narrow):
                csend[c, j, r] = acc.astype(jnp.bfloat16)
                if j < narrow - 1:
                    acc = decay(t1, j, c * rows + r) * acc + got1[c, j, r].astype(jnp.float32)
        begin(4, c, lambda j: csend.at[c, j], lambda j: carried.at[c, j], near, group_at, n)
        carried[c, n] = csend[c, n]

    def stage5(c):
        arrive(4, c, lambda j: carried.at[c, j], near, group_at)

        def body(j, _):
            finish(c, j)
            return 0

        lax.fori_loop(0, narrow, body, 0, unroll=2)

    def totals1():
        arrive_total(0, t1, near, group_at)
        group_total = t1[0]
        for j in range(1, narrow):
            group_total = group_total + t1[j]
        t2[y] = group_total
        begin_total(1, t2, y, level, row_at)

    def totals2():
        arrive_total(1, t2, level, row_at)
        row_total = t2[0]
        for j in range(1, rows):
            row_total = row_total + t2[j]
        t3[z] = row_total
        begin_total(2, t3, z, deep, depth_at)

    pl.semaphore_wait(barrier, len(peers))
    begin_total(0, t1, n, near, group_at)
    loads[0].wait()
    loads[1].wait()
    for c in range(chunks):
        stage0(c)
    totals1()
    loads[2].wait()

    groups = heads // unit
    events = [(TIMES[p] + GAP * c, p, c) for p in range(5) for c in range(chunks)]
    events += [(TIMES[1] - 0.1, 5, 0), (TIMES[2] - 0.1, 6, 0)]
    early = min(groups, EARLY)
    within(0, early)
    filled = early
    for _, p, c in sorted(events):
        if p == 4 and filled < groups:
            within(filled, groups)
            filled = groups
        if p == 5:
            totals2()
        elif p == 6:
            arrive_total(2, t3, deep, depth_at)
        else:
            (stage1, stage2, stage3, stage4, stage5)[p](c)
            if filled < groups:
                within(filled, filled + 1)
                filled += 1
    for one in pending:
        one.wait_send()


TIMES = (5.4, 7.8, 12.8, 15.2, 19.6)
GAP = 2.75
EARLY = 2


def on_device(mesh_sizes, queries, keys, values, log_decay, gain):
    outer, narrow = mesh_sizes
    tokens, model = queries.shape
    heads = log_decay.shape[0]
    width = model // heads
    depth, rows = split_outer(outer)
    own = heads // narrow
    chunks = own // rows
    unit = min(4, own)
    half = lambda *shape: pltpu.VMEM(shape + (width, width), jnp.bfloat16)
    full = lambda *shape: pltpu.VMEM(shape, jnp.float32)
    most = max(narrow, depth, rows)
    dma = lambda *shape: pltpu.SemaphoreType.DMA(shape)
    vmem = pl.BlockSpec(memory_space=pltpu.VMEM)
    hbm = pl.BlockSpec(memory_space=pltpu.HBM)
    return pl.pallas_call(
        functools.partial(kernel, (narrow, depth, rows, heads, width, unit)),
        out_shape=jax.ShapeDtypeStruct(queries.shape, jnp.bfloat16),
        in_specs=[hbm] * 3 + [vmem] * 2,
        out_specs=vmem,
        scratch_shapes=[
            pltpu.VMEM((tokens, model), queries.dtype),
            pltpu.VMEM((tokens, model), queries.dtype),
            pltpu.VMEM((tokens, model), queries.dtype),
            full(heads, tokens),
            full(heads // unit, tokens, 128),
            full(heads // unit, tokens, 128),
            full(heads // unit, tokens, 128),
            full(tokens, tokens),
            full(tokens, model),
            half(chunks, narrow, rows),
            half(chunks, narrow, rows),
            full(narrow, heads, width),
            half(chunks, rows),
            half(chunks, rows),
            full(rows, heads, width),
            half(chunks, depth),
            full(depth, heads, width),
            half(chunks, rows),
            half(chunks, rows),
            half(chunks, narrow, rows),
            half(chunks, narrow, rows),
            dma(3),
            dma(5, chunks, most),
            dma(5, chunks, most),
            dma(3, most),
            dma(3, most),
        ],
        compiler_params=pltpu.CompilerParams(
            collective_id=0, has_side_effects=True, vmem_limit_bytes=48 * 1024 * 1024
        ),
    )(queries, keys, values, log_decay, gain.reshape(1, model))


def solution(mesh):
    axes = ("outer", "narrow")
    block = P(axes, None)
    return jax.shard_map(
        functools.partial(on_device, tuple(mesh.shape[a] for a in axes)),
        mesh=mesh,
        in_specs=(block, block, block, P(None, axes), P()),
        out_specs=block,
        check_vma=False,
    )
```

profile of v0, /device:TPU:1, one launch (start us, length us, event | category | flops | bytes accessed | tf_op | source)
XLA Modules:
  0.0 42.8 jit_solution(12882221686801072213)
XLA Ops:
  0.0 0.0 copy-start
  0.0 1.6 %copy-done = bf16[256,4096]{1,0:T(8,128)(2,1)S(1)} copy-done((bf16[256,4096]{1,0:T(8,128)(2,1)S(1)}, bf16[256,4096]{1,0:T(8,128)(2,1)}, u32[]{:S(2)}) %copy-start) | copy-done | bytes 2097176
  1.6 0.0 copy-start.1
  1.6 0.8 %copy-done.1 = f32[32,256]{1,0:T(8,128)S(1)} copy-done((f32[32,256]{1,0:T(8,128)S(1)}, f32[32,256]{1,0:T(8,128)}, u32[]{:S(2)}) %copy-start.1) | copy-done | bytes 32792
  2.4 0.0 copy-start.2
  2.4 0.7 %copy-done.2 = f32[4096]{0:T(1024)S(1)} copy-done((f32[4096]{0:T(1024)S(1)}, f32[4096]{0:T(1024)}, u32[]{:S(2)}) %copy-start.2) | copy-done | bytes 16408
  3.1 38.4 %shard_map.55 = bf16[256,4096]{1,0:T(8,128)(2,1)S(1)} custom-call(bf16[256,4096]{1,0:T(8,128)(2,1)S(1)} %copy-done, bf16[256,4096]{1,0:T(8,128)(2,1)} %k_hbm.1, bf16[256,4096]{1,0:T(8,128)(2,1)} %v_hbm.1, f32[32,256]{1,0:T(8,128)S(1)} %copy-done.1, f32[1,4096]{1,0:T(1,128)S(1)} %bitcast.1), custom_call_target="tpu_custom_call" | custom-call | tf_op jit(solution)/shard_map/pallas_call | solution.py:282
  41.5 1.3 %copy.7 = bf16[256,4096]{1,0:T(8,128)(2,1)} copy(bf16[256,4096]{1,0:T(8,128)(2,1)S(1)} %shard_map.55) | data formatting | bytes 4194304
Async XLA Ops:
  0.0 1.6 %copy-start = (bf16[256,4096]{1,0:T(8,128)(2,1)S(1)}, bf16[256,4096]{1,0:T(8,128)(2,1)}, u32[]{:S(2)}) copy-start(bf16[256,4096]{1,0:T(8,128)(2,1)} %q_hbm.1) | copy-start | bytes 6291460
  1.6 0.8 %copy-start.1 = (f32[32,256]{1,0:T(8,128)S(1)}, f32[32,256]{1,0:T(8,128)}, u32[]{:S(2)}) copy-start(f32[32,256]{1,0:T(8,128)} %ld_ref.1) | copy-start | bytes 98308
  2.4 0.7 %copy-start.2 = (f32[4096]{0:T(1024)S(1)}, f32[4096]{0:T(1024)}, u32[]{:S(2)}) copy-start(f32[4096]{0:T(1024)} %param.9) | copy-start | bytes 49156
where the time goes:
time: 43.1 us; the launch traced here: 42.8 us
  Pallas kernels  38.4 us (89%)
  local copies, waits for them, and re-layouts  4.39 us (10%)
    pallas_call x1, Pallas kernels, on_device(): pl.pallas_call(functools.partial(kernel, (narrow, depth, rows, heads, wid...  38.4 us
    unnamed x7, local copies, waits for them, and re-layouts  4.39 us

commit v1 on v0

--- a/solution.py
+++ b/solution.py
@@ -20,10 +20,10 @@
 
 
 def kernel(
-    sizes, q_hbm, k_hbm, v_hbm, ld_ref, gain_ref, out_ref,
-    q_ref, k_ref, v_ref, cum, decay_cols, tail_cols, head_cols, bias, inner,
+    sizes, q_hbm, k_hbm, v_hbm, ld_hbm, gain_hbm, out_hbm,
+    q_ref, k_ref, v_ref, ld_ref, gain_ref, out_ref, cum, decay_cols, tail_cols, head_cols, bias, inner,
     made, got1, t1, wsend, got2, t2, got3, t3, gsend, got4, csend, carried,
-    load_sem, send_sem, recv_sem, tsend_sem, trecv_sem,
+    load_sem, out_sem, send_sem, recv_sem, tsend_sem, trecv_sem,
 ):
     narrow, depth, rows, heads, width, unit = sizes
     tokens = q_ref.shape[0]
@@ -41,7 +41,9 @@
 
     loads = [
         pltpu.make_async_copy(src, dst, load_sem.at[i])
-        for i, (src, dst) in enumerate(((k_hbm, k_ref), (v_hbm, v_ref), (q_hbm, q_ref)))
+        for i, (src, dst) in enumerate(
+            ((ld_hbm, ld_ref), (k_hbm, k_ref), (v_hbm, v_ref), (q_hbm, q_ref), (gain_hbm, gain_ref))
+        )
     ]
     for one in loads:
         one.start()
@@ -51,6 +53,7 @@
     for peer in peers:
         pl.semaphore_signal(barrier, inc=1, device_id=peer, device_id_type=MESH)
 
+    loads[0].wait()
     total = ld_ref[...]
     lane = lax.broadcasted_iota(jnp.int32, total.shape, 1)
     step = 1
@@ -117,7 +120,7 @@
             mean = jnp.mean(numer * numer, axis=-1, keepdims=True)
             out_ref[:, at] = (numer * lax.rsqrt(mean + 1e-06) * gain_ref[:, at]).astype(jnp.bfloat16)
 
-    pending = []
+    pending, stored = [], []
 
     def begin(kind, c, src, dst, peers_of, where, mine):
         for i, j in enumerate(peers_of):
@@ -210,6 +213,11 @@
             return 0
 
         lax.fori_loop(0, narrow, body, 0, unroll=2)
+        for j in range(narrow):
+            at = pl.ds((j * own + c * rows) * width, rows * width)
+            one = pltpu.make_async_copy(out_ref.at[:, at], out_hbm.at[:, at], out_sem.at[c, j])
+            one.start()
+            stored.append(one)
 
     def totals1():
         arrive_total(0, t1, near, group_at)
@@ -229,12 +237,13 @@
 
     pl.semaphore_wait(barrier, len(peers))
     begin_total(0, t1, n, near, group_at)
-    loads[0].wait()
     loads[1].wait()
+    loads[2].wait()
     for c in range(chunks):
         stage0(c)
     totals1()
-    loads[2].wait()
+    loads[3].wait()
+    loads[4].wait()
 
     groups = heads // unit
     events = [(TIMES[p] + GAP * c, p, c) for p in range(5) for c in range(chunks)]
@@ -257,6 +266,8 @@
                 filled += 1
     for one in pending:
         one.wait_send()
+    for one in stored:
+        one.wait()
 
 
 TIMES = (5.4, 7.8, 12.8, 15.2, 19.6)
@@ -277,16 +288,18 @@
     full = lambda *shape: pltpu.VMEM(shape, jnp.float32)
     most = max(narrow, depth, rows)
     dma = lambda *shape: pltpu.SemaphoreType.DMA(shape)
-    vmem = pl.BlockSpec(memory_space=pltpu.VMEM)
     hbm = pl.BlockSpec(memory_space=pltpu.HBM)
     return pl.pallas_call(
         functools.partial(kernel, (narrow, depth, rows, heads, width, unit)),
         out_shape=jax.ShapeDtypeStruct(queries.shape, jnp.bfloat16),
-        in_specs=[hbm] * 3 + [vmem] * 2,
-        out_specs=vmem,
+        in_specs=[hbm] * 5,
+        out_specs=hbm,
         scratch_shapes=[
             pltpu.VMEM((tokens, model), queries.dtype),
             pltpu.VMEM((tokens, model), queries.dtype),
+            pltpu.VMEM((tokens, model), queries.dtype),
+            full(heads, tokens),
+            full(1, model),
             pltpu.VMEM((tokens, model), queries.dtype),
             full(heads, tokens),
             full(heads // unit, tokens, 128),
@@ -306,14 +319,15 @@
             half(chunks, rows),
             half(chunks, narrow, rows),
             half(chunks, narrow, rows),
-            dma(3),
+            dma(5),
+            dma(chunks, narrow),
             dma(5, chunks, most),
             dma(5, chunks, most),
             dma(3, most),
             dma(3, most),
         ],
         compiler_params=pltpu.CompilerParams(
-            collective_id=0, has_side_effects=True, vmem_limit_bytes=48 * 1024 * 1024
+            collective_id=0, has_side_effects=True, vmem_limit_bytes=67_000_000
         ),
     )(queries, keys, values, log_decay, gain.reshape(1, model))
 

time: 43.1 us -> 42.6 us (0.988)
  local copies, waits for them, and re-layouts: 4.39 us -> 3.13 us
  Pallas kernels: 38.4 us -> 39.3 us
    unnamed x7 -> x1, local copies, waits for them, and re-layouts: 4.39 us -> 3.13 us
    pallas_call x1, Pallas kernels: 38.4 us -> 39.3 us  [on_device(): pl.pallas_call(functools.partial(kernel, (narrow, depth, rows, heads, wid...]
where the time goes in v1:
time: 42.6 us; the launch traced here: 42.4 us
  Pallas kernels  39.3 us (92%)
  local copies, waits for them, and re-layouts  3.13 us (7%)
    pallas_call x1, Pallas kernels, on_device(): pl.pallas_call(functools.partial(kernel, (narrow, depth, rows, heads, wid...  39.3 us
    unnamed x1, local copies, waits for them, and re-layouts  3.13 us

profile of v1, /device:TPU:1, one launch (start us, length us, event | category | flops | bytes accessed | tf_op | source)
XLA Modules:
  0.0 42.4 jit_solution(10283929995489087401)
XLA Ops:
  0.0 39.3 %shard_map.55 = bf16[256,4096]{1,0:T(8,128)(2,1)} custom-call(bf16[256,4096]{1,0:T(8,128)(2,1)} %q_hbm.1, bf16[256,4096]{1,0:T(8,128)(2,1)} %k_hbm.1, bf16[256,4096]{1,0:T(8,128)(2,1)} %v_hbm.1, f32[32,256]{1,0:T(8,128)} %ld_hbm.1, f32[1,4096]{1,0:T(1,128)} %bitcast.1), custom_call_target="tpu_custom_call" | custom-call | tf_op jit(solution)/shard_map/pallas_call | solution.py:292
  39.3 3.1 %copy.7 = bf16[256,4096]{1,0:T(8,128)(2,1)} copy(bf16[256,4096]{1,0:T(8,128)(2,1)} %shard_map.55) | data formatting | bytes 4194304

commit v2 on v1

v2 whole, which is shorter than its diff:
```python
import functools

import jax
import jax.numpy as jnp
from jax import lax
from jax.experimental import pallas as pl
from jax.experimental.pallas import tpu as pltpu
from jax.sharding import PartitionSpec as P

MESH = pl.DeviceIdType.MESH
FAR = -1e30
CORES = 2
PARTS = 2
EARLY = 3
LAG_Z = 4
LAG_R = 8


def split_outer(outer):
    rows = 1
    for d in range(1, outer + 1):
        if d * d <= outer and outer % d == 0:
            rows = d
    return outer // rows, rows


def kernel(
    sizes, q_hbm, k_hbm, v_hbm, ld_hbm, gain_hbm, out_ref,
    q_ref, k_ref, v_ref, ld_ref, gain_ref, cum, decay_cols, tail_cols, bias, inner, grown,
    tcore, dcore, ptot, tin, dchip, tz, dz, down,
    made, pair, tsend, got_t, q_sum, zsend, got_z, rsend, got_r, own_c, csend, got_c,
    load_sem, made_send, made_recv, ct_send, ct_recv, t_send, t_recv, pt_send, pt_recv,
    zt_send, zt_recv, z_send, z_recv, r_send, r_recv, c_send, c_recv, ready,
):
    depth, rows, across, heads, width, per = sizes
    chips = rows * across
    levels = max(depth - 1, 1).bit_length() if depth > 1 else 0
    tokens = q_ref.shape[0]
    part = width // PARTS
    units = per * PARTS
    o, n = lax.axis_index("outer"), lax.axis_index("narrow")
    z, y = o // rows, lax.rem(o, rows)
    x, core = n // CORES, lax.rem(n, CORES)
    me = y * across + x
    first = core == 0

    partner = (o, x * CORES + 1 - core)
    chip_at = lambda p: (z * rows + p // across, lax.rem(p, across) * CORES + core)
    plane_at = lambda j: (j * rows + y, n)
    beside = lambda i: lax.rem(me + i, chips)
    slot = lambda p: lax.rem(p - me - 1 + chips, chips)

    loads = [
        pltpu.make_async_copy(src, dst, load_sem.at[i])
        for i, (src, dst) in enumerate(
            ((ld_hbm, ld_ref), (k_hbm, k_ref), (v_hbm, v_ref), (q_hbm, q_ref), (gain_hbm, gain_ref))
        )
    ]
    for one in loads:
        one.start()

    barrier = pltpu.get_barrier_semaphore()
    pl.semaphore_signal(barrier, inc=1, device_id=partner, device_id_type=MESH)
    for i in range(1, chips):
        pl.semaphore_signal(barrier, inc=1, device_id=chip_at(beside(i)), device_id_type=MESH)
    for j in range(1, depth):
        @pl.when(j > z)
        def _():
            pl.semaphore_signal(barrier, inc=1, device_id=plane_at(j), device_id_type=MESH)

    def remote(src, dst, send, recv, where):
        return pltpu.make_async_remote_copy(
            src_ref=src, dst_ref=dst, send_sem=send, recv_sem=recv, device_id=where, device_id_type=MESH
        )

    def arrived(ref, recv):
        remote(ref, ref, made_send, recv, partner).wait_recv()

    def sent(ref, send):
        remote(ref, ref, send, ct_recv, partner).wait_send()

    loads[0].wait()
    total = ld_ref[...]
    lane = lax.broadcasted_iota(jnp.int32, total.shape, 1)
    step = 1
    while step < tokens:
        total = total + jnp.where(lane >= step, pltpu.roll(total, step, axis=1), 0.0)
        step *= 2
    cum[...] = total
    last = jnp.broadcast_to(total[:, tokens - 1 :], (heads, width))
    for g in range(heads // per):
        tcore[core, g, :per, :] = last[g * per : (g + 1) * per]
    cols = jnp.concatenate([total, jnp.zeros((128 - heads, tokens), jnp.float32)], axis=0).T
    tail = jnp.exp(cols[tokens - 1 :] - cols)
    for g in range(heads // per):
        shift = (128 - g * per) % 128
        tail_cols[g] = pltpu.roll(tail, shift, axis=1) if shift else tail

    def lanes(h):
        return pl.ds(pl.multiple_of(h * width, width), width)

    def state(c, p, a):
        g = p * CORES + a
        at = lanes(g * per + c)
        kept = k_ref[:, at].astype(jnp.float32) * tail_cols[g][:, c : c + 1]
        return lax.dot_general(
            kept.astype(jnp.bfloat16), v_ref[:, at], (((0,), (0,)), ((), ())),
            preferred_element_type=jnp.float32,
        ).astype(jnp.bfloat16)

    def states(c, mine):
        def body(p, _):
            made_here = state(c, p, core if mine else 1 - core)
            for f in range(PARTS):
                piece = made_here[f * part : (f + 1) * part]
                if mine:
                    pair[core, c, f, p] = piece
                else:
                    made[c, f, p] = piece
            return 0

        lax.fori_loop(0, chips, body, 0, unroll=2 if chips % 2 == 0 else 1)

    def meet(c):
        arrived(pair.at[1 - core, c], made_recv.at[c])
        for f in range(PARTS):
            for p in range(chips):
                decay = dcore[1, p, pl.ds(c, 1), :]
                value = decay * pair[0, c, f, p].astype(jnp.float32) + pair[1, c, f, p].astype(jnp.float32)
                tsend[c, f, slot(p)] = value.astype(jnp.bfloat16)
            for i in range(1, chips):
                remote(
                    tsend.at[c, f, i - 1], got_t.at[c, f, chips - 1 - i], t_send,
                    t_recv.at[c * PARTS + f], chip_at(beside(i)),
                ).start()

    def meet_totals():
        arrived(tcore.at[1 - core], ct_recv)
        for p in range(chips):
            here = [tcore[k, p * CORES + core] for k in range(CORES)]
            for k in range(CORES):
                dcore[k, p] = jnp.exp(here[k])
            ptot[slot(p)] = here[0] + here[1]
        for i in range(1, chips):
            remote(ptot.at[i - 1], tin.at[chips - 1 - i], pt_send, pt_recv, chip_at(beside(i))).start()

    def within(g):
        columns = decay_cols[g]
        for u in range(per):
            h = g * per + u
            at = lanes(h)
            spread_t = jnp.broadcast_to(columns[:, u : u + 1], (tokens, width))
            grown[h] = jnp.exp(spread_t)
            scores = lax.dot_general(
                q_ref[:, at], k_ref[:, at], (((1,), (1,)), ((), ())),
                preferred_element_type=jnp.float32,
            )
            spread = columns[:, u : u + 1] - cum[pl.ds(h, 1), :] + bias[...]
            weights = (scores * jnp.exp(spread)).astype(jnp.bfloat16)
            inner[:, at] = jnp.dot(weights, v_ref[:, at], preferred_element_type=jnp.float32)

    def send_level(level, s):
        for i in range(2**level):
            @pl.when(z + 1 + i < depth)
            def _():
                remote(
                    zsend.at[s], got_z.at[level, s], z_send.at[i], z_recv.at[level, s], plane_at(z + 1 + i)
                ).start()

    def sends_at(level):
        return lax.rem(z, 2 ** (level + 1)) == 2**level - 1

    def plane_totals():
        if chips > 1:
            arrived(tin.at[pl.ds(0, chips - 1)], pt_recv)
        tin[chips - 1] = ptot[chips - 1]
        whole = jnp.zeros_like(tz[0])
        for p in range(chips):
            here = tin[slot(p)]
            dchip[p] = jnp.exp(here)
            whole = whole + here
        tz[z] = whole
        down[...] = jnp.exp(whole)
        if depth > 1:
            @pl.when(z < depth - 1)
            def _():
                pl.semaphore_wait(ready, depth - 1 - z)
            for i in range(1, depth):
                @pl.when(z + i < depth)
                def _():
                    remote(tz.at[z], tz.at[z], zt_send.at[i - 1], zt_recv.at[z], plane_at(z + i)).start()

    def plane(s):
        c, f = s // PARTS, lax.rem(s, PARTS)
        if chips > 1:
            arrived(got_t.at[c, f, pl.ds(0, chips - 1)], t_recv.at[s])
        got_t[c, f, chips - 1] = tsend[c, f, chips - 1]
        acc = got_t[c, f, slot(0)].astype(jnp.float32)
        for p in range(1, chips):
            acc = dchip[p, pl.ds(c, 1), :] * acc + got_t[c, f, slot(p)].astype(jnp.float32)
        q_sum[s] = acc
        if levels:
            @pl.when(sends_at(0))
            def _():
                zsend[s] = acc.astype(jnp.bfloat16)
                send_level(0, s)

    def depth_totals():
        for j in range(depth - 1):
            @pl.when(j < z)
            def _():
                arrived(tz.at[j], zt_recv.at[j])
        for k in range(1, levels):
            start = z // 2**k * 2**k
            whole = jnp.zeros_like(tz[0])
            for j in range(depth - 1):
                whole = whole + jnp.where((j >= start) & (j < z), tz[j], 0.0)
            dz[k] = jnp.exp(whole)

    def scan(s):
        c, f = s // PARTS, lax.rem(s, PARTS)
        acc = jnp.zeros((part, width), jnp.float32)
        for k in range(levels):
            odd = lax.rem(z // 2**k, 2) == 1

            @pl.when(odd)
            def _():
                arrived(got_z.at[k, s], z_recv.at[k, s])

            came = got_z[k, s].astype(jnp.float32)
            if k:
                came = dz[k, pl.ds(c, 1), :] * came + acc
            acc = jnp.where(odd, came, acc)
            if k + 1 < levels:
                @pl.when(sends_at(k + 1))
                def _():
                    zsend[s] = (down[pl.ds(c, 1), :] * acc + q_sum[s]).astype(jnp.bfloat16)
                    send_level(k + 1, s)
        for p in range(chips):
            rsend[c, f, slot(p)] = acc.astype(jnp.bfloat16)
            if p < chips - 1:
                acc = dchip[p, pl.ds(c, 1), :] * acc + got_t[c, f, slot(p)].astype(jnp.float32)
        for i in range(1, chips):
            remote(
                rsend.at[c, f, i - 1], got_r.at[c, f, chips - 1 - i], r_send, r_recv.at[s], chip_at(beside(i))
            ).start()

    def back(s):
        c, f = s // PARTS, lax.rem(s, PARTS)
        if chips > 1:
            arrived(got_r.at[c, f, pl.ds(0, chips - 1)], r_recv.at[s])
        got_r[c, f, chips - 1] = rsend[c, f, chips - 1]
        for p in range(chips):
            before = got_r[c, f, slot(p)]
            after = dcore[0, p, pl.ds(c, 1), :] * before.astype(jnp.float32) + pair[0, c, f, p].astype(jnp.float32)
            after = after.astype(jnp.bfloat16)
            own_c[c, f, p] = jnp.where(first, before, after)
            csend[c, f, p] = jnp.where(first, after, before)
        remote(csend.at[c, f], got_c.at[c, f], c_send, c_recv.at[c], partner).start()

    def finish(c, ref, a):
        def body(p, _):
            h = (p * CORES + a) * per + c
            at = lanes(h)
            carried = jnp.concatenate([ref[c, f, p] for f in range(PARTS)], axis=0)
            read = jnp.dot(q_ref[:, at], carried, preferred_element_type=jnp.float32)
            numer = inner[:, at] + read * grown[h]
            mean = jnp.mean(numer * numer, axis=-1, keepdims=True)
            out_ref[:, at] = (numer * lax.rsqrt(mean + 1e-06) * gain_ref[:, at]).astype(jnp.bfloat16)
            return 0

        lax.fori_loop(0, chips, body, 0, unroll=2 if chips % 2 == 0 else 1)

    loads[1].wait()
    loads[2].wait()
    states(0, False)
    pl.semaphore_wait(barrier, chips + z)
    if depth > 1:
        for j in range(depth - 1):
            @pl.when(j < z)
            def _():
                pl.semaphore_signal(ready, inc=1, device_id=plane_at(j), device_id_type=MESH)
    remote(tcore.at[core], tcore.at[core], ct_send, ct_recv, partner).start()
    for c in range(per):
        if c:
            states(c, False)
        remote(made.at[c], pair.at[core, c], made_send, made_recv.at[c], partner).start()
        if c:
            meet(c - 1)
        states(c, True)
        if c == 0:
            meet_totals()
    meet(per - 1)

    for g in range(heads // per):
        shift = (128 - g * per) % 128
        decay_cols[g] = pltpu.roll(cols, shift, axis=1) if shift else cols
    at_t = lax.broadcasted_iota(jnp.int32, (tokens, tokens), 0)
    at_s = lax.broadcasted_iota(jnp.int32, (tokens, tokens), 1)
    bias[...] = jnp.where(at_t >= at_s, 0.0, FAR)
    loads[3].wait()
    loads[4].wait()

    groups = heads // per
    early = min(EARLY, groups)
    lax.fori_loop(0, early, lambda g, _: (within(g), 0)[1], 0)
    plane_totals()

    rank = jnp.int32(0)
    for k in range(levels):
        rank = jnp.where(z >= 2**k, k + 1, rank)
    lag_z = jnp.minimum(rank * LAG_Z, units)
    lag_r = lag_z + LAG_R
    lag_f = lag_r + PARTS - 1
    steps = lag_f + units

    def step_at(s, _):
        @pl.when(s + early < groups)
        def _():
            within(s + early)

        @pl.when(s < units)
        def _():
            plane(s)

        if levels:
            @pl.when(s == lag_z)
            def _():
                depth_totals()

        @pl.when((s >= lag_z) & (s < lag_z + units))
        def _():
            scan(s - lag_z)

        @pl.when((s >= lag_r) & (s < lag_r + units))
        def _():
            back(s - lag_r)

        t = s - lag_f
        for f in range(PARTS):
            @pl.when((t >= 0) & (lax.rem(t + PARTS, PARTS) == f))
            def _():
                c = t // PARTS
                if f == 0:
                    finish(c, own_c, core)
                if f == PARTS - 1:
                    arrived(got_c.at[c], c_recv.at[c])
                    finish(c, got_c, 1 - core)
        return 0

    most = max(groups - early, units)
    lax.fori_loop(0, jnp.maximum(steps, most), step_at, 0)

    sent(made, made_send)
    sent(tcore.at[core], ct_send)
    if chips > 1:
        sent(tsend.at[:, :, pl.ds(0, chips - 1)], t_send)
        sent(ptot.at[pl.ds(0, chips - 1)], pt_send)
        sent(rsend.at[:, :, pl.ds(0, chips - 1)], r_send)
    sent(csend, c_send)
    for i in range(1, depth):
        @pl.when(z + i < depth)
        def _():
            sent(tz.at[z], zt_send.at[i - 1])
    for level in range(levels):
        for i in range(2**level):
            @pl.when(sends_at(level) & (z + 1 + i < depth))
            def _():
                sent(zsend, z_send.at[i])


def on_device(mesh_sizes, queries, keys, values, log_decay, gain):
    outer, narrow = mesh_sizes
    tokens, model = queries.shape
    heads = log_decay.shape[0]
    width = model // heads
    depth, rows = split_outer(outer)
    across = narrow // CORES
    chips = rows * across
    per = heads // (chips * CORES)
    groups = heads // per
    levels = max((depth - 1).bit_length(), 1)
    part = width // PARTS
    units = per * PARTS
    lines = -(-per // 8) * 8
    half = lambda *shape: pltpu.VMEM(shape, jnp.bfloat16)
    full = lambda *shape: pltpu.VMEM(shape, jnp.float32)
    dma = lambda *shape: pltpu.SemaphoreType.DMA(shape)
    one = pltpu.SemaphoreType.DMA
    vmem = pl.BlockSpec(memory_space=pltpu.VMEM)
    hbm = pl.BlockSpec(memory_space=pltpu.HBM)
    return pl.pallas_call(
        functools.partial(kernel, (depth, rows, across, heads, width, per)),
        out_shape=jax.ShapeDtypeStruct(queries.shape, jnp.bfloat16),
        in_specs=[hbm] * 5,
        out_specs=vmem,
        scratch_shapes=[
            pltpu.VMEM((tokens, model), queries.dtype),
            pltpu.VMEM((tokens, model), queries.dtype),
            pltpu.VMEM((tokens, model), queries.dtype),
            full(heads, tokens),
            full(1, model),
            full(heads, tokens),
            full(groups, tokens, 128),
            full(groups, tokens, 128),
            full(tokens, tokens),
            full(tokens, model),
            full(heads, tokens, width),
            full(CORES, groups, lines, width),
            full(CORES, chips, lines, width),
            full(chips, lines, width),
            full(chips, lines, width),
            full(chips, lines, width),
            full(depth, lines, width),
            full(levels, lines, width),
            full(lines, width),
            half(per, PARTS, chips, part, width),
            half(CORES, per, PARTS, chips, part, width),
            half(per, PARTS, chips, part, width),
            half(per, PARTS, chips, part, width),
            full(units, part, width),
            half(units, part, width),
            half(levels, units, part, width),
            half(per, PARTS, chips, part, width),
            half(per, PARTS, chips, part, width),
            half(per, PARTS, chips, part, width),
            half(per, PARTS, chips, part, width),
            half(per, PARTS, chips, part, width),
            dma(5),
            one, dma(per), one, one, one, dma(units), one, one,
            dma(max(depth - 1, 1)), dma(depth), dma(max(depth // 2, 1)), dma(levels, units),
            one, dma(units), one, dma(per),
            pltpu.SemaphoreType.REGULAR,
        ],
        compiler_params=pltpu.CompilerParams(
            collective_id=0, has_side_effects=True, vmem_limit_bytes=50 * 1024 * 1024
        ),
    )(queries, keys, values, log_decay, gain.reshape(1, model))


def solution(mesh):
    axes = ("outer", "narrow")
    block = P(axes, None)
    return jax.shard_map(
        functools.partial(on_device, tuple(mesh.shape[a] for a in axes)),
        mesh=mesh,
        in_specs=(block, block, block, P(None, axes), P()),
        out_specs=block,
        check_vma=False,
    )
```

time: 42.6 us -> 32.8 us (0.77)
  the two profiles are of different devices: /device:TPU:1 before, /device:TPU:25 now
where the time goes in v2:
time: 32.8 us; the launch traced here: 32.5 us
  Pallas kernels  29.7 us (91%)
  local copies, waits for them, and re-layouts  2.8 us (9%)
    pallas_call x1, Pallas kernels, on_device(): pl.pallas_call(functools.partial(kernel, (depth, rows, across, heads, wid...  29.7 us
    unnamed x5, local copies, waits for them, and re-layouts  2.8 us

profile of v2, /device:TPU:25, one launch (start us, length us, event | category | flops | bytes accessed | tf_op | source)
XLA Modules:
  0.0 32.5 jit_solution(15104491932127124661)
XLA Ops:
  0.0 0.0 copy-start
  0.0 0.8 %copy-done = f32[32,256]{1,0:T(8,128)S(1)} copy-done((f32[32,256]{1,0:T(8,128)S(1)}, f32[32,256]{1,0:T(8,128)}, u32[]{:S(2)}) %copy-start) | copy-done | bytes 32792
  0.8 0.0 copy-start.1
  0.8 0.7 %copy-done.1 = f32[4096]{0:T(1024)S(1)} copy-done((f32[4096]{0:T(1024)S(1)}, f32[4096]{0:T(1024)}, u32[]{:S(2)}) %copy-start.1) | copy-done | bytes 16408
  1.5 29.7 %shard_map.55 = bf16[256,4096]{1,0:T(8,128)(2,1)S(1)} custom-call(bf16[256,4096]{1,0:T(8,128)(2,1)} %q_hbm.1, bf16[256,4096]{1,0:T(8,128)(2,1)} %k_hbm.1, bf16[256,4096]{1,0:T(8,128)(2,1)} %v_hbm.1, f32[32,256]{1,0:T(8,128)S(1)} %copy-done, f32[1,4096]{1,0:T(1,128)S(1)} %bitcast.1), custom_call_target="tpu_custom_call" | custom-call | tf_op jit(solution)/shard_map/pallas_call | solution.py:392
  31.2 1.3 %copy.7 = bf16[256,4096]{1,0:T(8,128)(2,1)} copy(bf16[256,4096]{1,0:T(8,128)(2,1)S(1)} %shard_map.55) | data formatting | bytes 4194304
Async XLA Ops:
  0.0 0.8 %copy-start = (f32[32,256]{1,0:T(8,128)S(1)}, f32[32,256]{1,0:T(8,128)}, u32[]{:S(2)}) copy-start(f32[32,256]{1,0:T(8,128)} %ld_hbm.1) | copy-start | bytes 98308
  0.8 0.7 %copy-start.1 = (f32[4096]{0:T(1024)S(1)}, f32[4096]{0:T(1024)}, u32[]{:S(2)}) copy-start(f32[4096]{0:T(1024)} %param.9) | copy-start | bytes 49156

commit v3 on v2

--- a/solution.py
+++ b/solution.py
@@ -11,9 +11,8 @@
 FAR = -1e30
 CORES = 2
 PARTS = 2
-EARLY = 3
-LAG_Z = 4
-LAG_R = 8
+LAG_Z = 3
+LAG_R = 6
 
 
 def split_outer(outer):
@@ -26,10 +25,10 @@
 
 def kernel(
     sizes, q_hbm, k_hbm, v_hbm, ld_hbm, gain_hbm, out_ref,
-    q_ref, k_ref, v_ref, ld_ref, gain_ref, cum, decay_cols, tail_cols, bias, inner, grown,
+    q_ref, k_ref, v_ref, ld_ref, gain_ref, cum, cols_ref, tail_ref, bias, inner, grown,
     tcore, dcore, ptot, tin, dchip, tz, dz, down,
     made, pair, tsend, got_t, q_sum, zsend, got_z, rsend, got_r, own_c, csend, got_c,
-    load_sem, made_send, made_recv, ct_send, ct_recv, t_send, t_recv, pt_send, pt_recv,
+    load_sem, kv_sem, made_send, made_recv, ct_send, ct_recv, t_send, t_recv, pt_send, pt_recv,
     zt_send, zt_recv, z_send, z_recv, r_send, r_recv, c_send, c_recv, ready,
 ):
     depth, rows, across, heads, width, per = sizes
@@ -38,6 +37,8 @@
     tokens = q_ref.shape[0]
     part = width // PARTS
     units = per * PARTS
+    unit = 4 if heads % 4 == 0 else 1
+    groups = heads // unit
     o, n = lax.axis_index("outer"), lax.axis_index("narrow")
     z, y = o // rows, lax.rem(o, rows)
     x, core = n // CORES, lax.rem(n, CORES)
@@ -50,14 +51,28 @@
     beside = lambda i: lax.rem(me + i, chips)
     slot = lambda p: lax.rem(p - me - 1 + chips, chips)
 
+    def lanes(h, count=1):
+        return pl.ds(pl.multiple_of(h * width, width), count * width)
+
+    span = chips * CORES
     loads = [
         pltpu.make_async_copy(src, dst, load_sem.at[i])
-        for i, (src, dst) in enumerate(
-            ((ld_hbm, ld_ref), (k_hbm, k_ref), (v_hbm, v_ref), (q_hbm, q_ref), (gain_hbm, gain_ref))
-        )
+        for i, (src, dst) in enumerate(((ld_hbm, ld_ref), (q_hbm, q_ref), (gain_hbm, gain_ref)))
     ]
-    for one in loads:
-        one.start()
+
+    def load_kv(c):
+        at = lanes(c * span, span)
+        return [
+            pltpu.make_async_copy(src.at[:, at], dst.at[:, at], kv_sem.at[c, i])
+            for i, (src, dst) in enumerate(((k_hbm, k_ref), (v_hbm, v_ref)))
+        ]
+
+    loads[0].start()
+    for c in range(per):
+        for one in load_kv(c):
+            one.start()
+    loads[1].start()
+    loads[2].start()
 
     barrier = pltpu.get_barrier_semaphore()
     pl.semaphore_signal(barrier, inc=1, device_id=partner, device_id_type=MESH)
@@ -88,38 +103,33 @@
         step *= 2
     cum[...] = total
     last = jnp.broadcast_to(total[:, tokens - 1 :], (heads, width))
-    for g in range(heads // per):
-        tcore[core, g, :per, :] = last[g * per : (g + 1) * per]
+    for c in range(per):
+        for g in range(span):
+            h = c * span + g
+            tcore[core, g, c : c + 1, :] = last[h : h + 1]
     cols = jnp.concatenate([total, jnp.zeros((128 - heads, tokens), jnp.float32)], axis=0).T
-    tail = jnp.exp(cols[tokens - 1 :] - cols)
-    for g in range(heads // per):
-        shift = (128 - g * per) % 128
-        tail_cols[g] = pltpu.roll(tail, shift, axis=1) if shift else tail
-
-    def lanes(h):
-        return pl.ds(pl.multiple_of(h * width, width), width)
-
-    def state(c, p, a):
-        g = p * CORES + a
-        at = lanes(g * per + c)
-        kept = k_ref[:, at].astype(jnp.float32) * tail_cols[g][:, c : c + 1]
-        return lax.dot_general(
-            kept.astype(jnp.bfloat16), v_ref[:, at], (((0,), (0,)), ((), ())),
-            preferred_element_type=jnp.float32,
-        ).astype(jnp.bfloat16)
+    cols_ref[...] = cols
+    tail_ref[...] = jnp.exp(cols[tokens - 1 :] - cols)
+    at_t = lax.broadcasted_iota(jnp.int32, (width, width), 0)
+    at_s = lax.broadcasted_iota(jnp.int32, (width, width), 1)
+    bias[...] = jnp.where(at_t >= at_s, 0.0, FAR)
 
     def states(c, mine):
-        def body(p, _):
-            made_here = state(c, p, core if mine else 1 - core)
+        a = core if mine else 1 - core
+        tails = pltpu.roll(tail_ref[...], lax.rem(128 - (c * span + a), 128), axis=1)
+        for p in range(chips):
+            at = lanes(c * span + p * CORES + a)
+            kept = k_ref[:, at].astype(jnp.float32) * tails[:, p * CORES : p * CORES + 1]
+            made_here = lax.dot_general(
+                kept.astype(jnp.bfloat16), v_ref[:, at], (((0,), (0,)), ((), ())),
+                preferred_element_type=jnp.float32,
+            ).astype(jnp.bfloat16)
             for f in range(PARTS):
                 piece = made_here[f * part : (f + 1) * part]
                 if mine:
                     pair[core, c, f, p] = piece
                 else:
                     made[c, f, p] = piece
-            return 0
-
-        lax.fori_loop(0, chips, body, 0, unroll=2 if chips % 2 == 0 else 1)
 
     def meet(c):
         arrived(pair.at[1 - core, c], made_recv.at[c])
@@ -145,18 +155,32 @@
             remote(ptot.at[i - 1], tin.at[chips - 1 - i], pt_send, pt_recv, chip_at(beside(i))).start()
 
     def within(g):
-        columns = decay_cols[g]
-        for u in range(per):
-            h = g * per + u
+        columns = pltpu.roll(cols_ref[...], lax.rem(128 - g * unit, 128), axis=1)
+        for u in range(unit):
+            h = g * unit + u
             at = lanes(h)
-            spread_t = jnp.broadcast_to(columns[:, u : u + 1], (tokens, width))
-            grown[h] = jnp.exp(spread_t)
+            column = jnp.broadcast_to(columns[:, u : u + 1], (tokens, width))
+            grown[h] = jnp.exp(column)
+            row = cum[pl.ds(h, 1), :]
             scores = lax.dot_general(
                 q_ref[:, at], k_ref[:, at], (((1,), (1,)), ((), ())),
                 preferred_element_type=jnp.float32,
             )
-            spread = columns[:, u : u + 1] - cum[pl.ds(h, 1), :] + bias[...]
-            weights = (scores * jnp.exp(spread)).astype(jnp.bfloat16)
+            weights = []
+            for t in range(tokens // width):
+                rows_t = slice(t * width, (t + 1) * width)
+                line = []
+                for i in range(tokens // width):
+                    at_i = slice(i * width, (i + 1) * width)
+                    if i > t:
+                        line.append(jnp.zeros((width, width), jnp.bfloat16))
+                        continue
+                    spread = column[rows_t] - row[:, at_i]
+                    if i == t:
+                        spread = spread + bias[...]
+                    line.append((scores[rows_t, at_i] * jnp.exp(spread)).astype(jnp.bfloat16))
+                weights.append(jnp.concatenate(line, axis=1))
+            weights = jnp.concatenate(weights, axis=0)
             inner[:, at] = jnp.dot(weights, v_ref[:, at], preferred_element_type=jnp.float32)
 
     def send_level(level, s):
@@ -259,51 +283,48 @@
         remote(csend.at[c, f], got_c.at[c, f], c_send, c_recv.at[c], partner).start()
 
     def finish(c, ref, a):
-        def body(p, _):
-            h = (p * CORES + a) * per + c
+        for p in range(chips):
+            h = c * span + p * CORES + a
             at = lanes(h)
             carried = jnp.concatenate([ref[c, f, p] for f in range(PARTS)], axis=0)
             read = jnp.dot(q_ref[:, at], carried, preferred_element_type=jnp.float32)
             numer = inner[:, at] + read * grown[h]
             mean = jnp.mean(numer * numer, axis=-1, keepdims=True)
             out_ref[:, at] = (numer * lax.rsqrt(mean + 1e-06) * gain_ref[:, at]).astype(jnp.bfloat16)
-            return 0
-
-        lax.fori_loop(0, chips, body, 0, unroll=2 if chips % 2 == 0 else 1)
-
+
+    def make(c, _):
+        for one in load_kv(c):
+            one.wait()
+        states(c, False)
+
+        @pl.when(c == 0)
+        def _():
+            pl.semaphore_wait(barrier, chips + z)
+            for j in range(depth - 1):
+                @pl.when(j < z)
+                def _():
+                    pl.semaphore_signal(ready, inc=1, device_id=plane_at(j), device_id_type=MESH)
+            remote(tcore.at[core], tcore.at[core], ct_send, ct_recv, partner).start()
+
+        remote(made.at[c], pair.at[core, c], made_send, made_recv.at[c], partner).start()
+
+        @pl.when(c > 0)
+        def _():
+            meet(c - 1)
+
+        states(c, True)
+
+        @pl.when(c == 0)
+        def _():
+            meet_totals()
+
+        return 0
+
+    lax.fori_loop(0, per, make, 0)
     loads[1].wait()
     loads[2].wait()
-    states(0, False)
-    pl.semaphore_wait(barrier, chips + z)
-    if depth > 1:
-        for j in range(depth - 1):
-            @pl.when(j < z)
-            def _():
-                pl.semaphore_signal(ready, inc=1, device_id=plane_at(j), device_id_type=MESH)
-    remote(tcore.at[core], tcore.at[core], ct_send, ct_recv, partner).start()
-    for c in range(per):
-        if c:
-            states(c, False)
-        remote(made.at[c], pair.at[core, c], made_send, made_recv.at[c], partner).start()
-        if c:
-            meet(c - 1)
-        states(c, True)
-        if c == 0:
-            meet_totals()
+    within(0)
     meet(per - 1)
-
-    for g in range(heads // per):
-        shift = (128 - g * per) % 128
-        decay_cols[g] = pltpu.roll(cols, shift, axis=1) if shift else cols
-    at_t = lax.broadcasted_iota(jnp.int32, (tokens, tokens), 0)
-    at_s = lax.broadcasted_iota(jnp.int32, (tokens, tokens), 1)
-    bias[...] = jnp.where(at_t >= at_s, 0.0, FAR)
-    loads[3].wait()
-    loads[4].wait()
-
-    groups = heads // per
-    early = min(EARLY, groups)
-    lax.fori_loop(0, early, lambda g, _: (within(g), 0)[1], 0)
     plane_totals()
 
     rank = jnp.int32(0)
@@ -312,13 +333,9 @@
     lag_z = jnp.minimum(rank * LAG_Z, units)
     lag_r = lag_z + LAG_R
     lag_f = lag_r + PARTS - 1
-    steps = lag_f + units
+    steps = jnp.maximum(lag_f + units, groups - 1)
 
     def step_at(s, _):
-        @pl.when(s + early < groups)
-        def _():
-            within(s + early)
-
         @pl.when(s < units)
         def _():
             plane(s)
@@ -346,10 +363,14 @@
                 if f == PARTS - 1:
                     arrived(got_c.at[c], c_recv.at[c])
                     finish(c, got_c, 1 - core)
+
+        @pl.when(s + 1 < groups)
+        def _():
+            within(s + 1)
+
         return 0
 
-    most = max(groups - early, units)
-    lax.fori_loop(0, jnp.maximum(steps, most), step_at, 0)
+    lax.fori_loop(0, steps, step_at, 0)
 
     sent(made, made_send)
     sent(tcore.at[core], ct_send)
@@ -389,6 +410,7 @@
     one = pltpu.SemaphoreType.DMA
     vmem = pl.BlockSpec(memory_space=pltpu.VMEM)
     hbm = pl.BlockSpec(memory_space=pltpu.HBM)
+    arrays = (queries, keys, values, log_decay, gain.reshape(1, model))
     return pl.pallas_call(
         functools.partial(kernel, (depth, rows, across, heads, width, per)),
         out_shape=jax.ShapeDtypeStruct(queries.shape, jnp.bfloat16),
@@ -401,9 +423,9 @@
             full(heads, tokens),
             full(1, model),
             full(heads, tokens),
-            full(groups, tokens, 128),
-            full(groups, tokens, 128),
-            full(tokens, tokens),
+            full(tokens, 128),
+            full(tokens, 128),
+            full(width, width),
             full(tokens, model),
             full(heads, tokens, width),
             full(CORES, groups, lines, width),
@@ -426,7 +448,7 @@
             half(per, PARTS, chips, part, width),
             half(per, PARTS, chips, part, width),
             half(per, PARTS, chips, part, width),
-            dma(5),
+            dma(3), dma(per, 2),
             one, dma(per), one, one, one, dma(units), one, one,
             dma(max(depth - 1, 1)), dma(depth), dma(max(depth // 2, 1)), dma(levels, units),
             one, dma(units), one, dma(per),
@@ -435,7 +457,7 @@
         compiler_params=pltpu.CompilerParams(
             collective_id=0, has_side_effects=True, vmem_limit_bytes=50 * 1024 * 1024
         ),
-    )(queries, keys, values, log_decay, gain.reshape(1, model))
+    )(*(pltpu.with_memory_space_constraint(a, pltpu.HBM) for a in arrays))
 
 
 def solution(mesh):

time: 32.8 us -> 27.2 us (0.83)
  Pallas kernels: 29.7 us -> 25.7 us
  local copies, waits for them, and re-layouts: 2.8 us -> 1.32 us
    pallas_call x1, Pallas kernels: 29.7 us -> 25.7 us  [on_device(): pl.pallas_call(functools.partial(kernel, (depth, rows, across, heads, wid...]
    unnamed x5 -> x1, local copies, waits for them, and re-layouts: 2.8 us -> 1.32 us
where the time goes in v3:
time: 27.2 us; the launch traced here: 27 us
  Pallas kernels  25.7 us (94%)
  local copies, waits for them, and re-layouts  1.32 us (5%)
    pallas_call x1, Pallas kernels, on_device(): pl.pallas_call(functools.partial(kernel, (depth, rows, across, heads, wid...  25.7 us
    unnamed x1, local copies, waits for them, and re-layouts  1.32 us

profile of v3, /device:TPU:25, one launch (start us, length us, event | category | flops | bytes accessed | tf_op | source)
XLA Modules:
  0.0 27.0 jit_solution(5672252989266765122)
XLA Ops:
  0.0 25.7 %shard_map.55 = bf16[256,4096]{1,0:T(8,128)(2,1)S(1)} custom-call(bf16[256,4096]{1,0:T(8,128)(2,1)} %q_hbm.1, bf16[256,4096]{1,0:T(8,128)(2,1)} %k_hbm.1, bf16[256,4096]{1,0:T(8,128)(2,1)} %v_hbm.1, f32[32,256]{1,0:T(8,128)} %ld_hbm.1, f32[1,4096]{1,0:T(1,128)} %bitcast.1), custom_call_target="tpu_custom_call" | custom-call | tf_op jit(solution)/shard_map/pallas_call | solution.py:414
  25.7 1.3 %copy.7 = bf16[256,4096]{1,0:T(8,128)(2,1)} copy(bf16[256,4096]{1,0:T(8,128)(2,1)S(1)} %shard_map.55) | data formatting | bytes 4194304

commit v4 on v3

--- a/solution.py
+++ b/solution.py
@@ -25,7 +25,7 @@
 
 def kernel(
     sizes, q_hbm, k_hbm, v_hbm, ld_hbm, gain_hbm, out_ref,
-    q_ref, k_ref, v_ref, ld_ref, gain_ref, cum, cols_ref, tail_ref, bias, inner, grown,
+    q_ref, k_ref, v_ref, ld_ref, gain_ref, cum, cols_ref, tail_ref, side_ref, bias, inner, grown,
     tcore, dcore, ptot, tin, dchip, tz, dz, down,
     made, pair, tsend, got_t, q_sum, zsend, got_z, rsend, got_r, own_c, csend, got_c,
     load_sem, kv_sem, made_send, made_recv, ct_send, ct_recv, t_send, t_recv, pt_send, pt_recv,
@@ -68,11 +68,8 @@
         ]
 
     loads[0].start()
-    for c in range(per):
-        for one in load_kv(c):
-            one.start()
-    loads[1].start()
-    loads[2].start()
+    for one in load_kv(0):
+        one.start()
 
     barrier = pltpu.get_barrier_semaphore()
     pl.semaphore_signal(barrier, inc=1, device_id=partner, device_id_type=MESH)
@@ -95,6 +92,11 @@
         remote(ref, ref, send, ct_recv, partner).wait_send()
 
     loads[0].wait()
+    for c in range(1, per):
+        for one in load_kv(c):
+            one.start()
+    loads[1].start()
+    loads[2].start()
     total = ld_ref[...]
     lane = lax.broadcasted_iota(jnp.int32, total.shape, 1)
     step = 1
@@ -109,17 +111,20 @@
             tcore[core, g, c : c + 1, :] = last[h : h + 1]
     cols = jnp.concatenate([total, jnp.zeros((128 - heads, tokens), jnp.float32)], axis=0).T
     cols_ref[...] = cols
-    tail_ref[...] = jnp.exp(cols[tokens - 1 :] - cols)
+    tail = jnp.exp(cols[tokens - 1 :] - cols)
+    tail_ref[...] = pltpu.roll(tail, lax.rem(128 - core, 128), axis=1)
+    side_ref[...] = pltpu.roll(tail, 127 + core, axis=1)
     at_t = lax.broadcasted_iota(jnp.int32, (width, width), 0)
     at_s = lax.broadcasted_iota(jnp.int32, (width, width), 1)
     bias[...] = jnp.where(at_t >= at_s, 0.0, FAR)
 
     def states(c, mine):
         a = core if mine else 1 - core
-        tails = pltpu.roll(tail_ref[...], lax.rem(128 - (c * span + a), 128), axis=1)
-        for p in range(chips):
+        tails = tail_ref if mine else side_ref
+        for p in range(chips):
+            u = c * span + p * CORES
             at = lanes(c * span + p * CORES + a)
-            kept = k_ref[:, at].astype(jnp.float32) * tails[:, p * CORES : p * CORES + 1]
+            kept = k_ref[:, at].astype(jnp.float32) * tails[:, u : u + 1]
             made_here = lax.dot_general(
                 kept.astype(jnp.bfloat16), v_ref[:, at], (((0,), (0,)), ((), ())),
                 preferred_element_type=jnp.float32,
@@ -155,13 +160,11 @@
             remote(ptot.at[i - 1], tin.at[chips - 1 - i], pt_send, pt_recv, chip_at(beside(i))).start()
 
     def within(g):
-        columns = pltpu.roll(cols_ref[...], lax.rem(128 - g * unit, 128), axis=1)
-        for u in range(unit):
-            h = g * unit + u
-            at = lanes(h)
-            column = jnp.broadcast_to(columns[:, u : u + 1], (tokens, width))
+        for h in range(g * unit, (g + 1) * unit):
+            at = slice(h * width, (h + 1) * width)
+            column = jnp.broadcast_to(cols_ref[:, h : h + 1], (tokens, width))
             grown[h] = jnp.exp(column)
-            row = cum[pl.ds(h, 1), :]
+            row = cum[h : h + 1, :]
             scores = lax.dot_general(
                 q_ref[:, at], k_ref[:, at], (((1,), (1,)), ((), ())),
                 preferred_element_type=jnp.float32,
@@ -292,48 +295,38 @@
             mean = jnp.mean(numer * numer, axis=-1, keepdims=True)
             out_ref[:, at] = (numer * lax.rsqrt(mean + 1e-06) * gain_ref[:, at]).astype(jnp.bfloat16)
 
-    def make(c, _):
+    for c in range(per):
         for one in load_kv(c):
             one.wait()
         states(c, False)
-
-        @pl.when(c == 0)
-        def _():
+        if c == 0:
             pl.semaphore_wait(barrier, chips + z)
             for j in range(depth - 1):
                 @pl.when(j < z)
                 def _():
                     pl.semaphore_signal(ready, inc=1, device_id=plane_at(j), device_id_type=MESH)
             remote(tcore.at[core], tcore.at[core], ct_send, ct_recv, partner).start()
-
         remote(made.at[c], pair.at[core, c], made_send, made_recv.at[c], partner).start()
-
-        @pl.when(c > 0)
-        def _():
+        if c:
             meet(c - 1)
-
         states(c, True)
-
-        @pl.when(c == 0)
-        def _():
+        if c == 0:
             meet_totals()
-
-        return 0
-
-    lax.fori_loop(0, per, make, 0)
     loads[1].wait()
     loads[2].wait()
     within(0)
     meet(per - 1)
     plane_totals()
 
+    slots = [g + g // 3 for g in range(groups - 1)]
+
     rank = jnp.int32(0)
     for k in range(levels):
         rank = jnp.where(z >= 2**k, k + 1, rank)
     lag_z = jnp.minimum(rank * LAG_Z, units)
-    lag_r = lag_z + LAG_R
+    lag_r = lag_z + jnp.where(rank == levels, min(LAG_R, units), units)
     lag_f = lag_r + PARTS - 1
-    steps = jnp.maximum(lag_f + units, groups - 1)
+    steps = jnp.maximum(lag_f + units + 2, max(slots, default=0) + 1)
 
     def step_at(s, _):
         @pl.when(s < units)
@@ -354,19 +347,22 @@
             back(s - lag_r)
 
         t = s - lag_f
-        for f in range(PARTS):
-            @pl.when((t >= 0) & (lax.rem(t + PARTS, PARTS) == f))
-            def _():
-                c = t // PARTS
-                if f == 0:
-                    finish(c, own_c, core)
-                if f == PARTS - 1:
-                    arrived(got_c.at[c], c_recv.at[c])
-                    finish(c, got_c, 1 - core)
-
-        @pl.when(s + 1 < groups)
-        def _():
-            within(s + 1)
+
+        @pl.when((t >= 0) & (t < units) & (lax.rem(t + units, PARTS) == 0))
+        def _():
+            finish(t // PARTS, own_c, core)
+
+        t = t - PARTS - 1
+
+        @pl.when((t >= 0) & (lax.rem(t + units, PARTS) == 0))
+        def _():
+            arrived(got_c.at[t // PARTS], c_recv.at[t // PARTS])
+            finish(t // PARTS, got_c, 1 - core)
+
+        for g in range(1, groups):
+            @pl.when(s == slots[g - 1])
+            def _():
+                within(g)
 
         return 0
 
@@ -425,6 +421,7 @@
             full(heads, tokens),
             full(tokens, 128),
             full(tokens, 128),
+            full(tokens, 128),
             full(width, width),
             full(tokens, model),
             full(heads, tokens, width),

time: 27.2 us -> 25.1 us (0.923)
  Pallas kernels: 25.7 us -> 23.7 us
    pallas_call x1, Pallas kernels: 25.7 us -> 23.7 us  [on_device(): pl.pallas_call(functools.partial(kernel, (depth, rows, across, heads, wid...]
where the time goes in v4:
time: 25.1 us; the launch traced here: 25 us
  Pallas kernels  23.7 us (94%)
  local copies, waits for them, and re-layouts  1.32 us (5%)
    pallas_call x1, Pallas kernels, on_device(): pl.pallas_call(functools.partial(kernel, (depth, rows, across, heads, wid...  23.7 us
    unnamed x1, local copies, waits for them, and re-layouts  1.32 us

profile of v4, /device:TPU:25, one launch (start us, length us, event | category | flops | bytes accessed | tf_op | source)
XLA Modules:
  0.0 25.0 jit_solution(15571493106514153134)
XLA Ops:
  0.0 23.7 %shard_map.55 = bf16[256,4096]{1,0:T(8,128)(2,1)S(1)} custom-call(bf16[256,4096]{1,0:T(8,128)(2,1)} %q_hbm.1, bf16[256,4096]{1,0:T(8,128)(2,1)} %k_hbm.1, bf16[256,4096]{1,0:T(8,128)(2,1)} %v_hbm.1, f32[32,256]{1,0:T(8,128)} %ld_hbm.1, f32[1,4096]{1,0:T(1,128)} %bitcast.1), custom_call_target="tpu_custom_call" | custom-call | tf_op jit(solution)/shard_map/pallas_call | solution.py:410
  23.7 1.3 %copy.7 = bf16[256,4096]{1,0:T(8,128)(2,1)} copy(bf16[256,4096]{1,0:T(8,128)(2,1)S(1)} %shard_map.55) | data formatting | bytes 4194304

commit v5 on v4

--- a/solution.py
+++ b/solution.py
@@ -11,8 +11,9 @@
 FAR = -1e30
 CORES = 2
 PARTS = 2
-LAG_Z = 3
+LAG_Z = 2
 LAG_R = 6
+BUSY = 3
 
 
 def split_outer(outer):
@@ -25,7 +26,7 @@
 
 def kernel(
     sizes, q_hbm, k_hbm, v_hbm, ld_hbm, gain_hbm, out_ref,
-    q_ref, k_ref, v_ref, ld_ref, gain_ref, cum, cols_ref, tail_ref, side_ref, bias, inner, grown,
+    q_ref, k_ref, v_ref, ld_ref, gain_ref, cum, cols_ref, grow_ref, tail_ref, side_ref, bias, inner, grown,
     tcore, dcore, ptot, tin, dchip, tz, dz, down,
     made, pair, tsend, got_t, q_sum, zsend, got_z, rsend, got_r, own_c, csend, got_c,
     load_sem, kv_sem, made_send, made_recv, ct_send, ct_recv, t_send, t_recv, pt_send, pt_recv,
@@ -48,8 +49,14 @@
     partner = (o, x * CORES + 1 - core)
     chip_at = lambda p: (z * rows + p // across, lax.rem(p, across) * CORES + core)
     plane_at = lambda j: (j * rows + y, n)
-    beside = lambda i: lax.rem(me + i, chips)
-    slot = lambda p: lax.rem(p - me - 1 + chips, chips)
+    beside = lambda i: lax.rem(y + i // across, rows) * across + lax.rem(x + i % across, across)
+    back_slot = lambda i: (-(i // across) % rows) * across + -i % across - 1
+    served = sorted(range(1, chips), key=lambda i: (-(i // across > 0) - (i % across > 0), i))
+
+    def slot(p):
+        i = lax.rem(p // across - y + rows, rows) * across + lax.rem(p % across - x + across, across)
+        return lax.rem(i - 1 + chips, chips)
+
 
     def lanes(h, count=1):
         return pl.ds(pl.multiple_of(h * width, width), count * width)
@@ -92,36 +99,44 @@
         remote(ref, ref, send, ct_recv, partner).wait_send()
 
     loads[0].wait()
+    cols = jnp.concatenate([ld_ref[...], jnp.zeros((128 - heads, tokens), jnp.float32)], axis=0).T
+    line = lax.broadcasted_iota(jnp.int32, cols.shape, 0)
+    step = 1
+    while step < tokens:
+        if step < 8:
+            moved = jnp.where(line >= step, pltpu.roll(cols, step, axis=0), 0.0)
+        else:
+            moved = jnp.concatenate([jnp.zeros((step, 128), jnp.float32), cols[: tokens - step]], axis=0)
+        cols = cols + moved
+        step *= 2
+    cols_ref[...] = cols
+    tail = jnp.exp(cols[tokens - 1 :] - cols)
+    side_ref[...] = pltpu.roll(tail, 127 + core, axis=1)
+    tail_ref[...] = pltpu.roll(tail, lax.rem(128 - core, 128), axis=1)
     for c in range(1, per):
         for one in load_kv(c):
             one.start()
     loads[1].start()
     loads[2].start()
-    total = ld_ref[...]
-    lane = lax.broadcasted_iota(jnp.int32, total.shape, 1)
-    step = 1
-    while step < tokens:
-        total = total + jnp.where(lane >= step, pltpu.roll(total, step, axis=1), 0.0)
-        step *= 2
-    cum[...] = total
-    last = jnp.broadcast_to(total[:, tokens - 1 :], (heads, width))
-    for c in range(per):
-        for g in range(span):
-            h = c * span + g
-            tcore[core, g, c : c + 1, :] = last[h : h + 1]
-    cols = jnp.concatenate([total, jnp.zeros((128 - heads, tokens), jnp.float32)], axis=0).T
-    cols_ref[...] = cols
-    tail = jnp.exp(cols[tokens - 1 :] - cols)
-    tail_ref[...] = pltpu.roll(tail, lax.rem(128 - core, 128), axis=1)
-    side_ref[...] = pltpu.roll(tail, 127 + core, axis=1)
-    at_t = lax.broadcasted_iota(jnp.int32, (width, width), 0)
-    at_s = lax.broadcasted_iota(jnp.int32, (width, width), 1)
-    bias[...] = jnp.where(at_t >= at_s, 0.0, FAR)
-
-    def states(c, mine):
+
+    def decay_rows():
+        grow_ref[...] = jnp.exp(cols_ref[...])
+        total = cols_ref[...].T[:heads]
+        cum[...] = total
+        last = jnp.broadcast_to(total[:, tokens - 1 :], (heads, width))
+        for c in range(per):
+            for g in range(span):
+                h = c * span + g
+                tcore[core, g, c : c + 1, :] = last[h : h + 1]
+        remote(tcore.at[core], tcore.at[core], ct_send, ct_recv, partner).start()
+        at_t = lax.broadcasted_iota(jnp.int32, (width, width), 0)
+        at_s = lax.broadcasted_iota(jnp.int32, (width, width), 1)
+        bias[...] = jnp.where(at_t >= at_s, 0.0, FAR)
+
+    def states(c, mine, some=None):
         a = core if mine else 1 - core
         tails = tail_ref if mine else side_ref
-        for p in range(chips):
+        for p in some or range(chips):
             u = c * span + p * CORES
             at = lanes(c * span + p * CORES + a)
             kept = k_ref[:, at].astype(jnp.float32) * tails[:, u : u + 1]
@@ -143,9 +158,9 @@
                 decay = dcore[1, p, pl.ds(c, 1), :]
                 value = decay * pair[0, c, f, p].astype(jnp.float32) + pair[1, c, f, p].astype(jnp.float32)
                 tsend[c, f, slot(p)] = value.astype(jnp.bfloat16)
-            for i in range(1, chips):
+            for i in served:
                 remote(
-                    tsend.at[c, f, i - 1], got_t.at[c, f, chips - 1 - i], t_send,
+                    tsend.at[c, f, i - 1], got_t.at[c, f, back_slot(i)], t_send,
                     t_recv.at[c * PARTS + f], chip_at(beside(i)),
                 ).start()
 
@@ -157,13 +172,13 @@
                 dcore[k, p] = jnp.exp(here[k])
             ptot[slot(p)] = here[0] + here[1]
         for i in range(1, chips):
-            remote(ptot.at[i - 1], tin.at[chips - 1 - i], pt_send, pt_recv, chip_at(beside(i))).start()
+            remote(ptot.at[i - 1], tin.at[back_slot(i)], pt_send, pt_recv, chip_at(beside(i))).start()
 
     def within(g):
         for h in range(g * unit, (g + 1) * unit):
             at = slice(h * width, (h + 1) * width)
             column = jnp.broadcast_to(cols_ref[:, h : h + 1], (tokens, width))
-            grown[h] = jnp.exp(column)
+            grown[h] = jnp.broadcast_to(grow_ref[:, h : h + 1], (tokens, width))
             row = cum[h : h + 1, :]
             scores = lax.dot_general(
                 q_ref[:, at], k_ref[:, at], (((1,), (1,)), ((), ())),
@@ -267,9 +282,9 @@
             rsend[c, f, slot(p)] = acc.astype(jnp.bfloat16)
             if p < chips - 1:
                 acc = dchip[p, pl.ds(c, 1), :] * acc + got_t[c, f, slot(p)].astype(jnp.float32)
-        for i in range(1, chips):
+        for i in served:
             remote(
-                rsend.at[c, f, i - 1], got_r.at[c, f, chips - 1 - i], r_send, r_recv.at[s], chip_at(beside(i))
+                rsend.at[c, f, i - 1], got_r.at[c, f, back_slot(i)], r_send, r_recv.at[s], chip_at(beside(i))
             ).start()
 
     def back(s):
@@ -296,37 +311,45 @@
             out_ref[:, at] = (numer * lax.rsqrt(mean + 1e-06) * gain_ref[:, at]).astype(jnp.bfloat16)
 
     for c in range(per):
-        for one in load_kv(c):
-            one.wait()
-        states(c, False)
+        if c != 1:
+            for one in load_kv(c):
+                one.wait()
+        states(c, False, range(chips // 2 if c == 1 else 0, chips))
         if c == 0:
             pl.semaphore_wait(barrier, chips + z)
             for j in range(depth - 1):
                 @pl.when(j < z)
                 def _():
                     pl.semaphore_signal(ready, inc=1, device_id=plane_at(j), device_id_type=MESH)
-            remote(tcore.at[core], tcore.at[core], ct_send, ct_recv, partner).start()
         remote(made.at[c], pair.at[core, c], made_send, made_recv.at[c], partner).start()
-        if c:
+        if c == 0:
+            decay_rows()
+        if c > 1:
             meet(c - 1)
         states(c, True)
-        if c == 0:
+        if c == 0 and per > 1:
+            for one in load_kv(1):
+                one.wait()
+            states(1, False, range(chips // 2))
             meet_totals()
+            meet(0)
+    if per == 1:
+        meet_totals()
     loads[1].wait()
     loads[2].wait()
     within(0)
     meet(per - 1)
     plane_totals()
 
-    slots = [g + g // 3 for g in range(groups - 1)]
 
     rank = jnp.int32(0)
     for k in range(levels):
         rank = jnp.where(z >= 2**k, k + 1, rank)
-    lag_z = jnp.minimum(rank * LAG_Z, units)
+    lag_z = jnp.minimum(jnp.where(rank == levels, units, jnp.where(rank == 0, 2 * LAG_Z, LAG_Z)), units)
     lag_r = lag_z + jnp.where(rank == levels, min(LAG_R, units), units)
-    lag_f = lag_r + PARTS - 1
-    steps = jnp.maximum(lag_f + units + 2, max(slots, default=0) + 1)
+    inner_planes = rank == levels
+    slots = [jnp.where(inner_planes, g + g // 3, g if g < BUSY else max(g, units + LAG_Z + g - BUSY)) for g in range(groups - 1)]
+    steps = jnp.maximum(lag_r + units + 2, units + LAG_Z + groups)
 
     def step_at(s, _):
         @pl.when(s < units)
@@ -346,18 +369,19 @@
         def _():
             back(s - lag_r)
 
-        t = s - lag_f
-
-        @pl.when((t >= 0) & (t < units) & (lax.rem(t + units, PARTS) == 0))
+        t = s - lag_r
+
+        @pl.when((t >= 0) & (t < units) & (lax.rem(t + units, PARTS) == PARTS - 1))
         def _():
             finish(t // PARTS, own_c, core)
 
-        t = t - PARTS - 1
-
-        @pl.when((t >= 0) & (lax.rem(t + units, PARTS) == 0))
-        def _():
-            arrived(got_c.at[t // PARTS], c_recv.at[t // PARTS])
-            finish(t // PARTS, got_c, 1 - core)
+        end = t == units + 1
+        c = jnp.where(end, per - 1, (t - 2 * PARTS) // PARTS)
+
+        @pl.when(end | ((t >= 2 * PARTS) & (t <= units) & (lax.rem(t + units, PARTS) == 0)))
+        def _():
+            arrived(got_c.at[c], c_recv.at[c])
+            finish(c, got_c, 1 - core)
 
         for g in range(1, groups):
             @pl.when(s == slots[g - 1])
@@ -422,6 +446,7 @@
             full(tokens, 128),
             full(tokens, 128),
             full(tokens, 128),
+            full(tokens, 128),
             full(width, width),
             full(tokens, model),
             full(heads, tokens, width),

time: 25.1 us -> 24.9 us (level)
  no operation moved by 1% of the time
where the time goes in v5:
time: 24.9 us; the launch traced here: 24.8 us
  Pallas kernels  23.5 us (94%)
  local copies, waits for them, and re-layouts  1.32 us (5%)
    pallas_call x1, Pallas kernels, on_device(): pl.pallas_call(functools.partial(kernel, (depth, rows, across, heads, wid...  23.5 us
    unnamed x1, local copies, waits for them, and re-layouts  1.32 us

profile of v5, /device:TPU:25, one launch (start us, length us, event | category | flops | bytes accessed | tf_op | source)
XLA Modules:
  0.0 24.8 jit_solution(915648457419231930)
XLA Ops:
  0.0 23.5 %shard_map.55 = bf16[256,4096]{1,0:T(8,128)(2,1)S(1)} custom-call(bf16[256,4096]{1,0:T(8,128)(2,1)} %q_hbm.1, bf16[256,4096]{1,0:T(8,128)(2,1)} %k_hbm.1, bf16[256,4096]{1,0:T(8,128)(2,1)} %v_hbm.1, f32[32,256]{1,0:T(8,128)} %ld_hbm.1, f32[1,4096]{1,0:T(1,128)} %bitcast.1), custom_call_target="tpu_custom_call" | custom-call | tf_op jit(solution)/shard_map/pallas_call | solution.py:434
  23.5 1.3 %copy.7 = bf16[256,4096]{1,0:T(8,128)(2,1)} copy(bf16[256,4096]{1,0:T(8,128)(2,1)S(1)} %shard_map.55) | data formatting | bytes 4194304

commit v6 on v5

--- a/solution.py
+++ b/solution.py
@@ -27,7 +27,7 @@
 def kernel(
     sizes, q_hbm, k_hbm, v_hbm, ld_hbm, gain_hbm, out_ref,
     q_ref, k_ref, v_ref, ld_ref, gain_ref, cum, cols_ref, grow_ref, tail_ref, side_ref, bias, inner, grown,
-    tcore, dcore, ptot, tin, dchip, tz, dz, down,
+    tcore, dcore, ptot, tin, dchip, tz, dz,
     made, pair, tsend, got_t, q_sum, zsend, got_z, rsend, got_r, own_c, csend, got_c,
     load_sem, kv_sem, made_send, made_recv, ct_send, ct_recv, t_send, t_recv, pt_send, pt_recv,
     zt_send, zt_recv, z_send, z_recv, r_send, r_recv, c_send, c_recv, ready,
@@ -110,6 +110,7 @@
         cols = cols + moved
         step *= 2
     cols_ref[...] = cols
+    tcore[core] = cols[tokens - 1 :]
     tail = jnp.exp(cols[tokens - 1 :] - cols)
     side_ref[...] = pltpu.roll(tail, 127 + core, axis=1)
     tail_ref[...] = pltpu.roll(tail, lax.rem(128 - core, 128), axis=1)
@@ -123,12 +124,6 @@
         grow_ref[...] = jnp.exp(cols_ref[...])
         total = cols_ref[...].T[:heads]
         cum[...] = total
-        last = jnp.broadcast_to(total[:, tokens - 1 :], (heads, width))
-        for c in range(per):
-            for g in range(span):
-                h = c * span + g
-                tcore[core, g, c : c + 1, :] = last[h : h + 1]
-        remote(tcore.at[core], tcore.at[core], ct_send, ct_recv, partner).start()
         at_t = lax.broadcasted_iota(jnp.int32, (width, width), 0)
         at_s = lax.broadcasted_iota(jnp.int32, (width, width), 1)
         bias[...] = jnp.where(at_t >= at_s, 0.0, FAR)
@@ -155,7 +150,7 @@
         arrived(pair.at[1 - core, c], made_recv.at[c])
         for f in range(PARTS):
             for p in range(chips):
-                decay = dcore[1, p, pl.ds(c, 1), :]
+                decay = dcore[c, p, 1:2, :]
                 value = decay * pair[0, c, f, p].astype(jnp.float32) + pair[1, c, f, p].astype(jnp.float32)
                 tsend[c, f, slot(p)] = value.astype(jnp.bfloat16)
             for i in served:
@@ -164,15 +159,25 @@
                     t_recv.at[c * PARTS + f], chip_at(beside(i)),
                 ).start()
 
+    def spread_rows(rows, first_lane):
+        count = -(-len(rows) // 8) * 8
+        rows = rows + [jnp.zeros((count - len(rows), 128), jnp.float32)] * (count > len(rows))
+        return pltpu.roll(jnp.exp(jnp.concatenate(rows, axis=0)), lax.rem(128 - first_lane, 128), axis=1)
+
     def meet_totals():
         arrived(tcore.at[1 - core], ct_recv)
+        for i in range(chips):
+            ptot[i] = tcore[0] + tcore[1]
+        for i in served:
+            remote(ptot.at[i - 1], tin.at[back_slot(i)], pt_send, pt_recv, chip_at(beside(i))).start()
+        rows = spread_rows([tcore[k] for k in range(CORES)], core)
+        pair_decays(rows, 0)
+        return rows
+
+    def pair_decays(rows, c):
         for p in range(chips):
-            here = [tcore[k, p * CORES + core] for k in range(CORES)]
-            for k in range(CORES):
-                dcore[k, p] = jnp.exp(here[k])
-            ptot[slot(p)] = here[0] + here[1]
-        for i in range(1, chips):
-            remote(ptot.at[i - 1], tin.at[back_slot(i)], pt_send, pt_recv, chip_at(beside(i))).start()
+            u = c * span + p * CORES
+            dcore[c, p] = jnp.broadcast_to(rows[:, u : u + 1], (8, width))
 
     def within(g):
         for h in range(g * unit, (g + 1) * unit):
@@ -216,13 +221,11 @@
         if chips > 1:
             arrived(tin.at[pl.ds(0, chips - 1)], pt_recv)
         tin[chips - 1] = ptot[chips - 1]
-        whole = jnp.zeros_like(tz[0])
-        for p in range(chips):
-            here = tin[slot(p)]
-            dchip[p] = jnp.exp(here)
-            whole = whole + here
+        rows = [tin[slot(p)] for p in range(chips)]
+        whole = rows[0]
+        for row in rows[1:]:
+            whole = whole + row
         tz[z] = whole
-        down[...] = jnp.exp(whole)
         if depth > 1:
             @pl.when(z < depth - 1)
             def _():
@@ -231,6 +234,9 @@
                 @pl.when(z + i < depth)
                 def _():
                     remote(tz.at[z], tz.at[z], zt_send.at[i - 1], zt_recv.at[z], plane_at(z + i)).start()
+        rows = spread_rows(rows + [whole], me * CORES + core)
+        for c in range(per):
+            dchip[c] = jnp.broadcast_to(rows[:, c * span : c * span + 1], (rows.shape[0], width))
 
     def plane(s):
         c, f = s // PARTS, lax.rem(s, PARTS)
@@ -239,7 +245,7 @@
         got_t[c, f, chips - 1] = tsend[c, f, chips - 1]
         acc = got_t[c, f, slot(0)].astype(jnp.float32)
         for p in range(1, chips):
-            acc = dchip[p, pl.ds(c, 1), :] * acc + got_t[c, f, slot(p)].astype(jnp.float32)
+            acc = dchip[c, p : p + 1, :] * acc + got_t[c, f, slot(p)].astype(jnp.float32)
         q_sum[s] = acc
         if levels:
             @pl.when(sends_at(0))
@@ -252,12 +258,16 @@
             @pl.when(j < z)
             def _():
                 arrived(tz.at[j], zt_recv.at[j])
+        rows = [jnp.zeros_like(tz[0])]
         for k in range(1, levels):
             start = z // 2**k * 2**k
             whole = jnp.zeros_like(tz[0])
             for j in range(depth - 1):
                 whole = whole + jnp.where((j >= start) & (j < z), tz[j], 0.0)
-            dz[k] = jnp.exp(whole)
+            rows.append(whole)
+        rows = spread_rows(rows, me * CORES + core)
+        for c in range(per):
+            dz[c] = jnp.broadcast_to(rows[:, c * span : c * span + 1], (rows.shape[0], width))
 
     def scan(s):
         c, f = s // PARTS, lax.rem(s, PARTS)
@@ -271,17 +281,17 @@
 
             came = got_z[k, s].astype(jnp.float32)
             if k:
-                came = dz[k, pl.ds(c, 1), :] * came + acc
+                came = dz[c, k : k + 1, :] * came + acc
             acc = jnp.where(odd, came, acc)
             if k + 1 < levels:
                 @pl.when(sends_at(k + 1))
                 def _():
-                    zsend[s] = (down[pl.ds(c, 1), :] * acc + q_sum[s]).astype(jnp.bfloat16)
+                    zsend[s] = (dchip[c, chips : chips + 1, :] * acc + q_sum[s]).astype(jnp.bfloat16)
                     send_level(k + 1, s)
         for p in range(chips):
             rsend[c, f, slot(p)] = acc.astype(jnp.bfloat16)
             if p < chips - 1:
-                acc = dchip[p, pl.ds(c, 1), :] * acc + got_t[c, f, slot(p)].astype(jnp.float32)
+                acc = dchip[c, p : p + 1, :] * acc + got_t[c, f, slot(p)].astype(jnp.float32)
         for i in served:
             remote(
                 rsend.at[c, f, i - 1], got_r.at[c, f, back_slot(i)], r_send, r_recv.at[s], chip_at(beside(i))
@@ -294,7 +304,7 @@
         got_r[c, f, chips - 1] = rsend[c, f, chips - 1]
         for p in range(chips):
             before = got_r[c, f, slot(p)]
-            after = dcore[0, p, pl.ds(c, 1), :] * before.astype(jnp.float32) + pair[0, c, f, p].astype(jnp.float32)
+            after = dcore[c, p, 0:1, :] * before.astype(jnp.float32) + pair[0, c, f, p].astype(jnp.float32)
             after = after.astype(jnp.bfloat16)
             own_c[c, f, p] = jnp.where(first, before, after)
             csend[c, f, p] = jnp.where(first, after, before)
@@ -317,12 +327,13 @@
         states(c, False, range(chips // 2 if c == 1 else 0, chips))
         if c == 0:
             pl.semaphore_wait(barrier, chips + z)
+            remote(tcore.at[core], tcore.at[core], ct_send, ct_recv, partner).start()
+        remote(made.at[c], pair.at[core, c], made_send, made_recv.at[c], partner).start()
+        if c == 0:
             for j in range(depth - 1):
                 @pl.when(j < z)
                 def _():
                     pl.semaphore_signal(ready, inc=1, device_id=plane_at(j), device_id_type=MESH)
-        remote(made.at[c], pair.at[core, c], made_send, made_recv.at[c], partner).start()
-        if c == 0:
             decay_rows()
         if c > 1:
             meet(c - 1)
@@ -331,15 +342,17 @@
             for one in load_kv(1):
                 one.wait()
             states(1, False, range(chips // 2))
-            meet_totals()
+            pair_rows = meet_totals()
             meet(0)
+            for later in range(1, per):
+                pair_decays(pair_rows, later)
     if per == 1:
         meet_totals()
     loads[1].wait()
     loads[2].wait()
+    plane_totals()
     within(0)
     meet(per - 1)
-    plane_totals()
 
 
     rank = jnp.int32(0)
@@ -349,7 +362,7 @@
     lag_r = lag_z + jnp.where(rank == levels, min(LAG_R, units), units)
     inner_planes = rank == levels
     slots = [jnp.where(inner_planes, g + g // 3, g if g < BUSY else max(g, units + LAG_Z + g - BUSY)) for g in range(groups - 1)]
-    steps = jnp.maximum(lag_r + units + 2, units + LAG_Z + groups)
+    steps = jnp.maximum(lag_r + units, units + LAG_Z + groups)
 
     def step_at(s, _):
         @pl.when(s < units)
@@ -371,15 +384,13 @@
 
         t = s - lag_r
 
-        @pl.when((t >= 0) & (t < units) & (lax.rem(t + units, PARTS) == PARTS - 1))
+        @pl.when((t >= 0) & (t < units - 1) & (lax.rem(t + units, PARTS) == PARTS - 1))
         def _():
             finish(t // PARTS, own_c, core)
 
-        end = t == units + 1
-        c = jnp.where(end, per - 1, (t - 2 * PARTS) // PARTS)
-
-        @pl.when(end | ((t >= 2 * PARTS) & (t <= units) & (lax.rem(t + units, PARTS) == 0)))
-        def _():
+        @pl.when((t >= 2 * PARTS) & (t < units - PARTS) & (lax.rem(t + units, PARTS) == 0))
+        def _():
+            c = (t - 2 * PARTS) // PARTS
             arrived(got_c.at[c], c_recv.at[c])
             finish(c, got_c, 1 - core)
 
@@ -391,6 +402,10 @@
         return 0
 
     lax.fori_loop(0, steps, step_at, 0)
+    finish(per - 1, own_c, core)
+    for c in range(max(per - 3, 0), per):
+        arrived(got_c.at[c], c_recv.at[c])
+        finish(c, got_c, 1 - core)
 
     sent(made, made_send)
     sent(tcore.at[core], ct_send)
@@ -423,7 +438,6 @@
     levels = max((depth - 1).bit_length(), 1)
     part = width // PARTS
     units = per * PARTS
-    lines = -(-per // 8) * 8
     half = lambda *shape: pltpu.VMEM(shape, jnp.bfloat16)
     full = lambda *shape: pltpu.VMEM(shape, jnp.float32)
     dma = lambda *shape: pltpu.SemaphoreType.DMA(shape)
@@ -450,14 +464,13 @@
             full(width, width),
             full(tokens, model),
             full(heads, tokens, width),
-            full(CORES, groups, lines, width),
-            full(CORES, chips, lines, width),
-            full(chips, lines, width),
-            full(chips, lines, width),
-            full(chips, lines, width),
-            full(depth, lines, width),
-            full(levels, lines, width),
-            full(lines, width),
+            full(CORES, 1, 128),
+            full(per, chips, 8, width),
+            full(chips, 1, 128),
+            full(chips, 1, 128),
+            full(per, -(-(chips + 1) // 8) * 8, width),
+            full(depth, 1, 128),
+            full(per, -(-levels // 8) * 8, width),
             half(per, PARTS, chips, part, width),
             half(CORES, per, PARTS, chips, part, width),
             half(per, PARTS, chips, part, width),

time: 24.9 us -> 24.6 us (0.988)
  Pallas kernels: 23.5 us -> 23.1 us
    pallas_call x1, Pallas kernels: 23.5 us -> 23.1 us  [on_device(): pl.pallas_call(functools.partial(kernel, (depth, rows, across, heads, wid...]
where the time goes in v6:
time: 24.6 us; the launch traced here: 24.5 us
  Pallas kernels  23.1 us (94%)
  local copies, waits for them, and re-layouts  1.32 us (5%)
    pallas_call x1, Pallas kernels, on_device(): pl.pallas_call(functools.partial(kernel, (depth, rows, across, heads, wid...  23.1 us
    unnamed x1, local copies, waits for them, and re-layouts  1.32 us

profile of v6, /device:TPU:25, one launch (start us, length us, event | category | flops | bytes accessed | tf_op | source)
XLA Modules:
  0.0 24.5 jit_solution(12036116619177430000)
XLA Ops:
  0.0 23.1 %shard_map.55 = bf16[256,4096]{1,0:T(8,128)(2,1)S(1)} custom-call(bf16[256,4096]{1,0:T(8,128)(2,1)} %q_hbm.1, bf16[256,4096]{1,0:T(8,128)(2,1)} %k_hbm.1, bf16[256,4096]{1,0:T(8,128)(2,1)} %v_hbm.1, f32[32,256]{1,0:T(8,128)} %ld_hbm.1, f32[1,4096]{1,0:T(1,128)} %bitcast.1), custom_call_target="tpu_custom_call" | custom-call | tf_op jit(solution)/shard_map/pallas_call | solution.py:448
  23.1 1.3 %copy.7 = bf16[256,4096]{1,0:T(8,128)(2,1)} copy(bf16[256,4096]{1,0:T(8,128)(2,1)S(1)} %shard_map.55) | data formatting | bytes 4194304

commit v7 on v6

--- a/solution.py
+++ b/solution.py
@@ -99,6 +99,9 @@
         remote(ref, ref, send, ct_recv, partner).wait_send()
 
     loads[0].wait()
+    if per > 1:
+        for one in load_kv(1):
+            one.start()
     cols = jnp.concatenate([ld_ref[...], jnp.zeros((128 - heads, tokens), jnp.float32)], axis=0).T
     line = lax.broadcasted_iota(jnp.int32, cols.shape, 0)
     step = 1
@@ -114,7 +117,7 @@
     tail = jnp.exp(cols[tokens - 1 :] - cols)
     side_ref[...] = pltpu.roll(tail, 127 + core, axis=1)
     tail_ref[...] = pltpu.roll(tail, lax.rem(128 - core, 128), axis=1)
-    for c in range(1, per):
+    for c in range(2, per):
         for one in load_kv(c):
             one.start()
     loads[1].start()
@@ -128,10 +131,10 @@
         at_s = lax.broadcasted_iota(jnp.int32, (width, width), 1)
         bias[...] = jnp.where(at_t >= at_s, 0.0, FAR)
 
-    def states(c, mine, some=None):
+    def states(c, mine):
         a = core if mine else 1 - core
         tails = tail_ref if mine else side_ref
-        for p in some or range(chips):
+        for p in range(chips):
             u = c * span + p * CORES
             at = lanes(c * span + p * CORES + a)
             kept = k_ref[:, at].astype(jnp.float32) * tails[:, u : u + 1]
@@ -320,40 +323,38 @@
             mean = jnp.mean(numer * numer, axis=-1, keepdims=True)
             out_ref[:, at] = (numer * lax.rsqrt(mean + 1e-06) * gain_ref[:, at]).astype(jnp.bfloat16)
 
-    for c in range(per):
-        if c != 1:
-            for one in load_kv(c):
-                one.wait()
-        states(c, False, range(chips // 2 if c == 1 else 0, chips))
+    def for_partner(c):
+        for one in load_kv(c):
+            one.wait()
+        states(c, False)
         if c == 0:
             pl.semaphore_wait(barrier, chips + z)
             remote(tcore.at[core], tcore.at[core], ct_send, ct_recv, partner).start()
         remote(made.at[c], pair.at[core, c], made_send, made_recv.at[c], partner).start()
-        if c == 0:
-            for j in range(depth - 1):
-                @pl.when(j < z)
-                def _():
-                    pl.semaphore_signal(ready, inc=1, device_id=plane_at(j), device_id_type=MESH)
-            decay_rows()
-        if c > 1:
-            meet(c - 1)
-        states(c, True)
-        if c == 0 and per > 1:
-            for one in load_kv(1):
-                one.wait()
-            states(1, False, range(chips // 2))
+
+    for_partner(0)
+    for j in range(depth - 1):
+        @pl.when(j < z)
+        def _():
+            pl.semaphore_signal(ready, inc=1, device_id=plane_at(j), device_id_type=MESH)
+    states(0, True)
+    for c in range(1, per):
+        for_partner(c)
+        if c == 1:
             pair_rows = meet_totals()
-            meet(0)
+        meet(c - 1)
+        if c == 1:
             for later in range(1, per):
                 pair_decays(pair_rows, later)
+        states(c, True)
     if per == 1:
         meet_totals()
+    decay_rows()
     loads[1].wait()
     loads[2].wait()
     plane_totals()
     within(0)
     meet(per - 1)
-
 
     rank = jnp.int32(0)
     for k in range(levels):
@@ -361,8 +362,8 @@
     lag_z = jnp.minimum(jnp.where(rank == levels, units, jnp.where(rank == 0, 2 * LAG_Z, LAG_Z)), units)
     lag_r = lag_z + jnp.where(rank == levels, min(LAG_R, units), units)
     inner_planes = rank == levels
-    slots = [jnp.where(inner_planes, g + g // 3, g if g < BUSY else max(g, units + LAG_Z + g - BUSY)) for g in range(groups - 1)]
-    steps = jnp.maximum(lag_r + units, units + LAG_Z + groups)
+    slots = [jnp.where(inner_planes, g + g // 3 if g < units - 3 else 2 * g, g if g < BUSY else max(g, units + LAG_Z + g - BUSY)) for g in range(groups - 1)]
+    steps = jnp.maximum(lag_r + units, max(units + LAG_Z + groups, 2 * groups))
 
     def step_at(s, _):
         @pl.when(s < units)

time: 24.6 us -> 23.9 us (0.972)
  Pallas kernels: 23.1 us -> 22.4 us
    pallas_call x1, Pallas kernels: 23.1 us -> 22.4 us  [on_device(): pl.pallas_call(functools.partial(kernel, (depth, rows, across, heads, wid...]
where the time goes in v7:
time: 23.9 us; the launch traced here: 23.7 us
  Pallas kernels  22.4 us (94%)
  local copies, waits for them, and re-layouts  1.32 us (6%)
    pallas_call x1, Pallas kernels, on_device(): pl.pallas_call(functools.partial(kernel, (depth, rows, across, heads, wid...  22.4 us
    unnamed x1, local copies, waits for them, and re-layouts  1.32 us

profile of v7, /device:TPU:25, one launch (start us, length us, event | category | flops | bytes accessed | tf_op | source)
XLA Modules:
  0.0 23.7 jit_solution(18355902849005555639)
XLA Ops:
  0.0 22.4 %shard_map.55 = bf16[256,4096]{1,0:T(8,128)(2,1)S(1)} custom-call(bf16[256,4096]{1,0:T(8,128)(2,1)} %q_hbm.1, bf16[256,4096]{1,0:T(8,128)(2,1)} %k_hbm.1, bf16[256,4096]{1,0:T(8,128)(2,1)} %v_hbm.1, f32[32,256]{1,0:T(8,128)} %ld_hbm.1, f32[1,4096]{1,0:T(1,128)} %bitcast.1), custom_call_target="tpu_custom_call" | custom-call | tf_op jit(solution)/shard_map/pallas_call | solution.py:449
  22.4 1.3 %copy.7 = bf16[256,4096]{1,0:T(8,128)(2,1)} copy(bf16[256,4096]{1,0:T(8,128)(2,1)S(1)} %shard_map.55) | data formatting | bytes 4194304

commit v8 on v7

--- a/solution.py
+++ b/solution.py
@@ -12,7 +12,7 @@
 CORES = 2
 PARTS = 2
 LAG_Z = 2
-LAG_R = 6
+LAG_R = 7
 BUSY = 3
 
 

time: 23.9 us -> 23.9 us (level)
  no operation moved by 1% of the time
where the time goes in v8:
time: 23.9 us; the launch traced here: 23.7 us
  Pallas kernels  22.4 us (94%)
  local copies, waits for them, and re-layouts  1.32 us (6%)
    pallas_call x1, Pallas kernels, on_device(): pl.pallas_call(functools.partial(kernel, (depth, rows, across, heads, wid...  22.4 us
    unnamed x1, local copies, waits for them, and re-layouts  1.32 us

profile of v8, /device:TPU:25, one launch (start us, length us, event | category | flops | bytes accessed | tf_op | source)
XLA Modules:
  0.0 23.7 jit_solution(17608762326105133758)
XLA Ops:
  0.0 22.4 %shard_map.55 = bf16[256,4096]{1,0:T(8,128)(2,1)S(1)} custom-call(bf16[256,4096]{1,0:T(8,128)(2,1)} %q_hbm.1, bf16[256,4096]{1,0:T(8,128)(2,1)} %k_hbm.1, bf16[256,4096]{1,0:T(8,128)(2,1)} %v_hbm.1, f32[32,256]{1,0:T(8,128)} %ld_hbm.1, f32[1,4096]{1,0:T(1,128)} %bitcast.1), custom_call_target="tpu_custom_call" | custom-call | tf_op jit(solution)/shard_map/pallas_call | solution.py:449
  22.4 1.3 %copy.7 = bf16[256,4096]{1,0:T(8,128)(2,1)} copy(bf16[256,4096]{1,0:T(8,128)(2,1)S(1)} %shard_map.55) | data formatting | bytes 4194304
